TPU v7x, 128 devices: a whole 4x4x4 slice. The times are simulated.
128 devices in a mesh: dp: 8 (over x, core), tp: 16 (over y, z).
Axes of the slice: x: 4, y: 4, z: 4, core: 2. Of those that a mesh axis runs over, the one named last changes fastest.
Arguments:
- queries: bfloat16 [1024, 128, 576], P(('dp', 'tp')), may hold values from -10 to 10
- new_latent: bfloat16 [1024, 576], P(('dp', 'tp')), may hold values from -6 to 6
- resident: bfloat16 [768, 256, 576], P(('dp', 'tp')), may hold values from -6 to 6
- leaving: bfloat16 [256, 2, 256, 576], P(('dp', 'tp')), may hold values from -6 to 6
- res_len: int32 [768], P(('dp', 'tp')), may hold values from 1 to 256, as said below
- leave_len: int32 [128, 2], replicated, may hold values from 1 to 256, as said below
- mig_dest: int32 [128, 2], replicated, may hold values from 0 to 15, as said below
- stream: bfloat16 [1024, 7168], P(('dp', 'tp')), may hold values from -6 to 6
- dense_gain: float32 [7168], replicated, may hold values from 0.1 to 1.9
- w_gate: bfloat16 [7168, 18432], P('dp', 'tp'), may hold values from -0.0625 to 0.0625
- w_up: bfloat16 [7168, 18432], P('dp', 'tp'), may hold values from -0.0625 to 0.0625
- w_down: bfloat16 [18432, 7168], P('tp', 'dp'), may hold values from -0.046875 to 0.046875
- moe_gain: float32 [7168], replicated, may hold values from 0.1 to 1.9
- expert_gate: bfloat16 [16, 7168, 2048], P('tp', None, 'dp'), may hold values from -0.0625 to 0.0625
- expert_up: bfloat16 [16, 7168, 2048], P('tp', None, 'dp'), may hold values from -0.0625 to 0.0625
- expert_down: bfloat16 [16, 2048, 7168], P('tp', 'dp'), may hold values from -0.125 to 0.125
- expert_ids: int32 [1024, 8], P(('dp', 'tp')), may hold values from 0 to 15, all different within a row; in each aligned block of 8 rows (0 to 7, 8 to 15, ...) at most 5 rows name the same one
- gate_scores: float32 [1024, 8], P(('dp', 'tp')), may hold values from 0.05 to 1
Outputs:
- context: bfloat16 [1024, 128, 512], P(('dp', 'tp'))
- arrived: bfloat16 [256, 2, 256, 576], P(('dp', 'tp'))
- stream_out: bfloat16 [1024, 7168], P(('dp', 'tp'))
Inputs may be any that keep to these rules, and one draw needn't show every extreme that they name: `mig_dest`: each device sends its 2 leaving requests to 2 different other devices of its dp index, and every device receives exactly 2 requests. `res_len`: some request holds all 256 positions. `leave_len`: some request holds all 256 positions. `expert_ids`: among the 8 rows of one device no expert is chosen by more than 5 rows, a bound that some block reaches; a row names 8 different experts.
All inputs are finite; a program needn't handle non-finite values.
Results may differ from a plain program's by a relative error of at most 0.023.
Values may be sent and summed in bfloat16 or wider, within the bound.
A program may use at most 128 MiB of HBM per device.

v0:
```python
import jax
import jax.numpy as jnp
from jax import lax
from jax.sharding import PartitionSpec as P

VDIM = 512
QKD = 192


EPS = 1e-06
ROUTE_SCALE = 2.5


def rms_scale(rows, gain):
    values = rows.astype(jnp.float32)
    mean_square = jnp.mean(values * values, axis=-1, keepdims=True)
    return (values * lax.rsqrt(mean_square + EPS) * gain).astype(jnp.bfloat16)


def attend(queries, keys, lengths, newest):
    scale = QKD ** (-0.5)
    scores = jnp.einsum("rhl,rcl->rhc", queries, keys, preferred_element_type=jnp.float32) * scale
    positions = jnp.arange(keys.shape[1])
    valid = positions[None, None, :] < lengths[:, None, None]
    masked = jnp.where(valid, scores, -1e30)
    own_score = (
        jnp.einsum("rhl,rl->rh", queries, newest, preferred_element_type=jnp.float32) * scale
    )
    top = jnp.maximum(jnp.max(masked, axis=-1), own_score)
    expo = jnp.where(valid, jnp.exp(masked - top[..., None]), 0.0)
    own_expo = jnp.exp(own_score - top)
    total = jnp.sum(expo, axis=-1) + own_expo
    weights = (expo / total[..., None]).astype(jnp.bfloat16)
    own_weight = (own_expo / total).astype(jnp.bfloat16)
    context = jnp.einsum(
        "rhc,rcv->rhv", weights, keys[:, :, :VDIM], preferred_element_type=jnp.float32
    )
    context = context + own_weight.astype(jnp.float32)[..., None] * newest[:, None, :VDIM].astype(
        jnp.float32
    )
    return context.astype(jnp.bfloat16)


def on_device(
    queries,
    new_latent,
    resident,
    leaving,
    res_len,
    leave_len,
    mig_dest,
    stream,
    dense_gain,
    w_gate,
    w_up,
    w_down,
    moe_gain,
    expert_gate,
    expert_up,
    expert_down,
    expert_ids,
    gate_scores,
):
    tp_count = lax.axis_size("tp")
    dp_count = lax.axis_size("dp")
    tp_rank = lax.axis_index("tp")
    dp_rank = lax.axis_index("dp")
    moving = leaving.shape[0]
    device = dp_rank * tp_count + tp_rank
    peers = jnp.arange(tp_count)
    own_dest = lax.dynamic_index_in_dim(mig_dest, device, 0, keepdims=False)
    outgoing = jnp.zeros((tp_count,) + leaving.shape[1:], jnp.bfloat16)
    for slot in range(moving):
        outgoing = jnp.where(
            (peers == own_dest[slot])[:, None, None, None], leaving[slot][None], outgoing
        )
    incoming = lax.all_to_all(outgoing, "tp", split_axis=0, concat_axis=0, tiled=True)
    group_dest = lax.dynamic_slice_in_dim(mig_dest, dp_rank * tp_count, tp_count, 0)
    group_len = lax.dynamic_slice_in_dim(leave_len, dp_rank * tp_count, tp_count, 0)
    match = group_dest == tp_rank
    is_source = jnp.any(match, axis=1)
    which = jnp.sum(jnp.where(match, jnp.arange(moving)[None, :], 0), axis=1)
    order = jnp.cumsum(is_source.astype(jnp.int32)) - 1
    arrivals = []
    arrival_len = []
    for arrival in range(moving):
        pick = is_source & (order == arrival)
        source = jnp.sum(jnp.where(pick, peers, 0))
        slot = jnp.sum(jnp.where(pick, which, 0))
        arrivals.append(lax.dynamic_index_in_dim(incoming, source, 0, keepdims=False))
        source_len = lax.dynamic_index_in_dim(group_len, source, 0, keepdims=False)
        arrival_len.append(lax.dynamic_index_in_dim(source_len, slot, 0, keepdims=False))
    arrived = jnp.stack(arrivals, axis=0)
    arrived_len = jnp.stack(arrival_len, axis=0)
    stay = resident.shape[0]
    context_stay = attend(queries[:stay], resident, res_len, new_latent[:stay])
    context_moved = attend(queries[stay:], arrived[:, 0], arrived_len, new_latent[stay:])
    context = jnp.concatenate([context_stay, context_moved], axis=0)
    rows_dev = stream.shape[0]
    width = stream.shape[1]
    normed = rms_scale(stream, dense_gain)
    nearby = lax.all_gather(normed[None], "tp", axis=0, tiled=True)
    gathered = lax.all_to_all(nearby[:, None], "dp", split_axis=3, concat_axis=1, tiled=True)
    features = gathered.reshape(-1, gathered.shape[-1])
    gate_part = jnp.dot(features, w_gate, preferred_element_type=jnp.float32)
    up_part = jnp.dot(features, w_up, preferred_element_type=jnp.float32)
    gate, up = (
        lax.psum(gate_part.astype(jnp.bfloat16), "dp").astype(jnp.float32),
        lax.psum(up_part.astype(jnp.bfloat16), "dp").astype(jnp.float32),
    )
    hidden_all = (jax.nn.silu(gate) * up).astype(jnp.bfloat16)
    block = hidden_all
    ffn_share = lax.psum_scatter(
        jnp.dot(block, w_down, preferred_element_type=jnp.float32).astype(jnp.bfloat16),
        "tp",
        scatter_dimension=0,
        tiled=True,
    ).astype(jnp.float32)
    ffn_rows = lax.all_to_all(
        ffn_share.reshape(dp_count, rows_dev, ffn_share.shape[-1]).astype(jnp.bfloat16),
        "dp",
        split_axis=0,
        concat_axis=2,
        tiled=True,
    ).astype(jnp.float32)
    middle = (stream.astype(jnp.float32) + ffn_rows[0]).astype(jnp.bfloat16)
    mixed = rms_scale(middle, moe_gain)
    experts = expert_gate.shape[0] * tp_count
    top_count = expert_ids.shape[1]
    capacity = min(rows_dev, rows_dev * top_count // experts + 1)
    hits = (expert_ids[:, :, None] == jnp.arange(experts)[None, None, :]).astype(jnp.int32)
    row_hits = jnp.sum(hits, axis=1)
    before = jnp.cumsum(row_hits, axis=0) - row_hits
    slot_of = jnp.sum(hits * before[:, None, :], axis=2)
    target = expert_ids * capacity + slot_of
    placed = jnp.any(target[:, :, None] == jnp.arange(experts * capacity)[None, None, :], axis=1)
    outgoing_rows = jnp.dot(
        placed.T.astype(jnp.bfloat16), mixed, preferred_element_type=jnp.float32
    )
    outgoing_rows = outgoing_rows.astype(jnp.bfloat16).reshape(experts, capacity, width)
    received = lax.all_to_all(outgoing_rows, "tp", split_axis=0, concat_axis=0, tiled=True)
    pooled = lax.all_gather(received, "dp", axis=0, tiled=True)
    flat = pooled.reshape(-1, width)
    block = flat
    gate = jnp.dot(block, expert_gate[0], preferred_element_type=jnp.float32)
    up = jnp.dot(block, expert_up[0], preferred_element_type=jnp.float32)
    inner = (jax.nn.silu(gate) * up).astype(jnp.bfloat16)
    summed = lax.psum_scatter(
        jnp.dot(inner, expert_down[0], preferred_element_type=jnp.float32).astype(jnp.bfloat16),
        "dp",
        scatter_dimension=0,
        tiled=True,
    )
    results = summed.reshape(received.shape)
    returned = lax.all_to_all(results, "tp", split_axis=0, concat_axis=0, tiled=True)
    flat_back = returned.reshape(experts * capacity, width)
    picked = jnp.take(flat_back, target.reshape(-1), axis=0).reshape(rows_dev, top_count, width)
    shares = gate_scores / jnp.sum(gate_scores, axis=1, keepdims=True) * ROUTE_SCALE
    routed = jnp.einsum("rk,rkd->rd", shares, picked.astype(jnp.float32))
    stream_out = (middle.astype(jnp.float32) + routed).astype(jnp.bfloat16)
    return (context, arrived, stream_out)


def solution(mesh):
    placed = (
        P(("dp", "tp"), None, None),
        P(("dp", "tp"), None),
        P(("dp", "tp"), None, None),
        P(("dp", "tp"), None, None, None),
        P(("dp", "tp")),
        P(),
        P(),
        P(("dp", "tp"), None),
        P(),
        P("dp", "tp"),
        P("dp", "tp"),
        P("tp", "dp"),
        P(),
        P("tp", None, "dp"),
        P("tp", None, "dp"),
        P("tp", "dp", None),
        P(("dp", "tp"), None),
        P(("dp", "tp"), None),
    )
    return jax.shard_map(
        on_device,
        mesh=mesh,
        in_specs=placed,
        out_specs=(
            P(("dp", "tp"), None, None),
            P(("dp", "tp"), None, None, None),
            P(("dp", "tp"), None),
        ),
        check_vma=False,
    )
```

profile of v0, /device:TPU:0, one launch (start us, length us, event | category | flops | bytes accessed | tf_op | source)
XLA Modules:
  0.0 688.6 jit_solution(10923640459823760998)
XLA Ops:
  8.4 1.6 fusion.51
  10.2 47.7 %all-gather.6.cloned.1.call-done = bf16[128,7168]{1,0:T(8,128)(2,1)} async-done(((bf16[8,7168]{1,0:T(8,128)(2,1)}), bf16[128,7168]{1,0:T(8,128)(2,1)}) %all-gather.6.cloned.1.call-update) | async-done | bytes 1835024 | tf_op jit(solution)/shard_map/all_gather | solution.py:102
  57.8 13.7 %copy.81 = bf16[16,1,8,7168]{0,2,1,3:T(8,128)(2,1)} copy(bf16[16,1,8,7168]{3,2,0,1:T(8,128)(2,1)} %bitcast.99) | data formatting | bytes 3670016 | tf_op jit(solution)/shard_map/broadcast_in_dim | solution.py:103
  71.6 17.3 %reshape.231 = bf16[8,2,57344]{2,1,0:T(2,128)(2,1)} reshape(bf16[7168,1,8,16]{3,2,1,0:T(8,128)(2,1)} %bitcast.94) | data formatting | bytes 3670016
  88.8 28.8 %all_to_all.39 = bf16[8,2,57344]{2,1,0:T(2,128)(2,1)} all-to-all(bf16[8,2,57344]{2,1,0:T(2,128)(2,1)} %reshape.231), channel_id=1, replica_groups=mesh['dp'=8,'tp'=16] {'dp'}, dimensions={0} | all-to-all | bytes 3670016 | tf_op jit(solution)/shard_map/all_to_all | solution.py:103
  117.6 12.5 %reshape.232 = bf16[7168,1,8,16]{3,2,1,0:T(8,128)(2,1)} reshape(bf16[8,2,57344]{2,1,0:T(2,128)(2,1)} %all_to_all.39) | data formatting | bytes 3670016
  130.1 13.8 %copy.95 = bf16[16,1,8,8,896]{4,3,2,0,1:T(8,128)(2,1)} copy(bf16[16,1,8,8,896]{0,2,4,3,1:T(8,128)(2,1)} %bitcast.95) | data formatting | bytes 3670016 | tf_op jit(solution)/shard_map/all_to_all | solution.py:103
  143.9 1.8 copy.83
  145.8 4.1 convolution_convert_fusion.2
  149.8 4.1 convolution_convert_fusion.3
  154.0 71.9 %all-reduce.3.cloned.1.call-done = (bf16[1024,1152]{1,0:T(8,128)(2,1)}, bf16[1024,1152]{1,0:T(8,128)(2,1)}) async-done(((bf16[1024,1152]{1,0:T(8,128)(2,1)}, bf16[1024,1152]{1,0:T(8,128)(2,1)}), (bf16[1024,1152]{1,0:T(8,128)(2,1)}, bf16[1024,1152]{1,0:T(8,128)(2,1)})) %all-reduce.3.cloned.1.call-update) | async-done | bytes 4718608 | tf_op jit(solution)/shard_map/psum | solution.py:109
  225.9 7.3 %fusion.12 = bf16[1024,896]{1,0:T(8,128)(2,1)} fusion(bf16[1152,896]{1,0:T(8,128)(2,1)} %param.29, bf16[1024,1152]{1,0:T(8,128)(2,1)} %get-tuple-element.30, bf16[1024,1152]{1,0:T(8,128)(2,1)} %get-tuple-element.31), kind=kOutput, calls=%fused_computation.19 | convolution fusion | flops 2124283904 | bytes 8617984 | tf_op jit(solution)/shard_map/dot_general | solution.py:114
  233.7 75.1 %reduce-scatter.3.cloned.1.call-done = bf16[64,896]{1,0:T(8,128)(2,1)} async-done(((bf16[1024,896]{1,0:T(8,128)(2,1)}), bf16[64,896]{1,0:T(8,128)(2,1)}) %reduce-scatter.3.cloned.1.call-update) | async-done | bytes 114704 | tf_op jit(solution)/shard_map/reduce_scatter | solution.py:113
  308.7 4.3 all-to-all-start.2
  313.3 5.6 all-to-all-done.2
  320.2 29.9 %all_to_all.40 = bf16[16,5,7168]{2,1,0:T(8,128)(2,1)S(1)} all-to-all(bf16[16,5,7168]{2,1,0:T(8,128)(2,1)S(1)} %reshape.205), channel_id=1, replica_groups=mesh['dp'=8,'tp'=16] {'tp'}, dimensions={0} | all-to-all | bytes 2293760 | tf_op jit(solution)/shard_map/all_to_all | solution.py:141
  350.2 1.8 copy.84
  352.0 49.3 %all-gather.4.cloned.1.call-done = bf16[128,5,7168]{2,0,1:T(8,128)(2,1)} async-done(((bf16[16,5,7168]{2,0,1:T(8,128)(2,1)}), bf16[128,5,7168]{2,0,1:T(8,128)(2,1)}) %all-gather.4.cloned.1.call-update) | async-done | bytes 9175056 | tf_op jit(solution)/shard_map/all_gather | solution.py:142
  401.3 14.0 %copy.85 = bf16[128,5,7168]{2,1,0:T(8,128)(2,1)} copy(bf16[128,5,7168]{2,0,1:T(8,128)(2,1)} %all-gather.4.cloned.1.call-done) | data formatting | bytes 18350080 | tf_op jit(solution)/shard_map/all_gather | solution.py:142
  415.3 15.1 %reshape.206 = bf16[640,7168]{1,0:T(8,128)(2,1)} reshape(bf16[128,5,7168]{2,1,0:T(8,128)(2,1)} %copy.85) | data formatting | bytes 18350080 | tf_op jit(solution)/shard_map/reshape | solution.py:143
  430.4 7.2 %fusion.8 = f32[640,256]{1,0:T(8,128)S(1)} fusion(bf16[640,7168]{1,0:T(8,128)(2,1)} %reshape.206, bf16[1,7168,256]{2,1,0:T(8,128)(2,1)} %param.31), kind=kOutput, calls=%fused_computation.16 | convolution fusion | flops 2348810240 | bytes 13500416 | tf_op jit(solution)/shard_map/dot_general | solution.py:145
  437.6 18.9 %convolution_convert_fusion = bf16[640,7168]{1,0:T(8,128)(2,1)} fusion(bf16[1,256,7168]{2,1,0:T(8,128)(2,1)} %param.33, bf16[640,7168]{1,0:T(8,128)(2,1)} %reshape.206, bf16[1,7168,256]{2,1,0:T(8,128)(2,1)} %param.32, f32[640,256]{1,0:T(8,128)S(1)} %fusion.8), kind=kOutput, calls=%fused_computation.1 | convolution fusion | flops 4703191040 | bytes 26345472 | tf_op jit(solution)/shard_map/dot_general | solution.py:149
  459.1 4.9 select_select_fusion
  464.1 7.2 %all-to-all-start = ((bf16[16,2,256,576]{2,3,1,0:T(8,128)(2,1)}), bf16[16,2,256,576]{2,3,1,0:T(8,128)(2,1)}, u32[]{:S(2)}, u32[]{:S(2)}) async-start(bf16[16,2,256,576]{2,3,1,0:T(8,128)(2,1)} %select_select_fusion), calls=%async_computation | async-start | bytes 18874368 | tf_op jit(solution)/shard_map/all_to_all | solution.py:77
  482.3 2.2 fusion.88
  485.3 1.6 add_convert_fusion
  486.9 148.7 %all-to-all-done = bf16[16,2,256,576]{2,3,1,0:T(8,128)(2,1)} async-done(((bf16[16,2,256,576]{2,3,1,0:T(8,128)(2,1)}), bf16[16,2,256,576]{2,3,1,0:T(8,128)(2,1)}, u32[]{:S(2)}, u32[]{:S(2)}) %all-to-all-start) | async-done | bytes 9437216 | tf_op jit(solution)/shard_map/all_to_all | solution.py:77
  638.1 2.6 reshape.207
  640.7 10.5 %all-to-all-start.4 = ((bf16[16,5,7168]{2,1,0:T(8,128)(2,1)}), bf16[16,5,7168]{2,1,0:T(8,128)(2,1)S(1)}, u32[]{:S(2)}, u32[]{:S(2)}) async-start(bf16[16,5,7168]{2,1,0:T(8,128)(2,1)} %reshape.207), calls=%async_computation.6 | async-start | bytes 3670016 | tf_op jit(solution)/shard_map/all_to_all | solution.py:155
  654.1 23.0 %all-to-all-done.4 = bf16[16,5,7168]{2,1,0:T(8,128)(2,1)S(1)} async-done(((bf16[16,5,7168]{2,1,0:T(8,128)(2,1)}), bf16[16,5,7168]{2,1,0:T(8,128)(2,1)S(1)}, u32[]{:S(2)}, u32[]{:S(2)}) %all-to-all-start.4) | async-done | bytes 1146912 | tf_op jit(solution)/shard_map/all_to_all | solution.py:155
  677.7 2.1 gather_fusion
  679.7 1.6 fusion.31
  (101 shorter events, 17.0 us)
Async XLA Ops:
  7.2 138.6 %copy-start = (bf16[896,1152]{1,0:T(8,128)(2,1)S(1)}, bf16[896,1152]{1,0:T(8,128)(2,1)}, u32[]{:S(2)}) copy-start(bf16[896,1152]{1,0:T(8,128)(2,1)} %param.28) | copy-start | bytes 6193156
  7.2 50.6 %all-gather.6.cloned.1.call-start = ((), (), s32[]{:S(2)}) async-start(), calls=%async_computation.10 | async-start | bytes 1949696 | tf_op jit(solution)/shard_map/all_gather | solution.py:102
  10.1 215.8 %all-reduce.3.cloned.1.call-start = ((), (), s32[]{:S(2)}) async-start(), calls=%async_computation.11 | async-start | bytes 9437184 | tf_op jit(solution)/shard_map/psum | solution.py:109
  145.7 4.1 copy-start.16
  154.0 154.8 %reduce-scatter.3.cloned.1.call-start = ((), (), s32[]{:S(2)}) async-start(), calls=%async_computation.7 | async-start | bytes 1949696 | tf_op jit(solution)/shard_map/reduce_scatter | solution.py:113
  225.9 7.4 %copy-start.10 = (s32[8,8]{1,0:T(8,128)S(1)}, s32[8,8]{1,0:T(8,128)}, u32[]{:S(2)}) copy-start(s32[8,8]{1,0:T(8,128)} %param.34) | copy-start | bytes 772
  233.2 85.7 %copy-start.4 = (bf16[8,7168]{1,0:T(8,128)(2,1)S(1)}, bf16[8,7168]{1,0:T(8,128)(2,1)}, u32[]{:S(2)}) copy-start(bf16[8,7168]{1,0:T(8,128)(2,1)} %param.25) | copy-start | bytes 344068
  233.2 85.9 %copy-start.11 = (f32[7168]{0:T(1024)S(1)}, f32[7168]{0:T(1024)}, u32[]{:S(2)}) copy-start(f32[7168]{0:T(1024)} %param.30) | copy-start | bytes 86020
  308.7 10.2 %all-to-all-start.2 = ((bf16[8,8,896]{2,1,0:T(8,128)(2,1)}), bf16[8,8,896]{2,1,0:T(8,128)(2,1)S(1)}, u32[]{:S(2)}, u32[]{:S(2)}) async-start(bf16[8,8,896]{2,1,0:T(8,128)(2,1)} %bitcast.101), calls=%async_computation.3 | async-start | bytes 229376 | tf_op jit(solution)/shard_map/all_to_all | solution.py:119
  313.0 88.3 %all-gather.4.cloned.1.call-start = ((), (), s32[]{:S(2)}) async-start(), calls=%async_computation.8 | async-start | bytes 10321920 | tf_op jit(solution)/shard_map/all_gather | solution.py:142
  351.9 286.2 %reduce-scatter.5.cloned.1.call-start = ((), (), s32[]{:S(2)}) async-start(), calls=%async_computation.9 | async-start | bytes 10321920 | tf_op jit(solution)/shard_map/reduce_scatter | solution.py:148
  456.5 0.7 copy-start.13
  456.5 2.6 copy-start.3
  464.0 15.9 %copy-start.12 = (f32[8,8]{1,0:T(8,128)S(1)}, f32[8,8]{1,0:T(8,128)}, u32[]{:S(2)}) copy-start(f32[8,8]{1,0:T(8,128)} %param.35) | copy-start | bytes 772
  464.0 16.0 %copy-start.14 = (s32[128,2]{0,1:T(2,128)S(1)}, s32[128,2]{0,1:T(2,128)}, u32[]{:S(2)}) copy-start(s32[128,2]{0,1:T(2,128)} %param.23) | copy-start | bytes 3076
  464.0 18.0 %copy-start.15 = (s32[6]{0:T(128)S(1)}, s32[6]{0:T(128)}, u32[]{:S(2)}) copy-start(s32[6]{0:T(128)} %param.22) | copy-start | bytes 76
  464.0 18.1 %copy-start.9 = (bf16[8,576]{1,0:T(8,128)(2,1)S(1)}, bf16[8,576]{1,0:T(8,128)(2,1)}, u32[]{:S(2)}) copy-start(bf16[8,576]{1,0:T(8,128)(2,1)} %param.19) | copy-start | bytes 27652
  464.1 18.1 %copy-start.2 = (bf16[8,128,576]{1,2,0:T(8,128)(2,1)S(1)}, bf16[8,128,576]{1,2,0:T(8,128)(2,1)}, u32[]{:S(2)}) copy-start(bf16[8,128,576]{1,2,0:T(8,128)(2,1)} %param.18) | copy-start | bytes 3538948
  464.1 171.5 %all-to-all-start = ((bf16[16,2,256,576]{2,3,1,0:T(8,128)(2,1)}), bf16[16,2,256,576]{2,3,1,0:T(8,128)(2,1)}, u32[]{:S(2)}, u32[]{:S(2)}) async-start(bf16[16,2,256,576]{2,3,1,0:T(8,128)(2,1)} %select_select_fusion), calls=%async_computation | async-start | bytes 18874368 | tf_op jit(solution)/shard_map/all_to_all | solution.py:77
  482.3 2.9 copy-start.17
  637.0 3.7 copy-start.6
  640.7 36.4 %all-to-all-start.4 = ((bf16[16,5,7168]{2,1,0:T(8,128)(2,1)}), bf16[16,5,7168]{2,1,0:T(8,128)(2,1)S(1)}, u32[]{:S(2)}, u32[]{:S(2)}) async-start(bf16[16,5,7168]{2,1,0:T(8,128)(2,1)} %reshape.207), calls=%async_computation.6 | async-start | bytes 3670016 | tf_op jit(solution)/shard_map/all_to_all | solution.py:155
  651.2 1.2 copy-start.8
  651.2 1.4 copy-start.7
  651.3 1.8 copy-start.5
  677.7 4.4 copy-start.1
Sparse Core Ops, SparseCore 0:
  10.7 47.0 all-gather.5
  154.1 71.7 all-reduce.2
  233.4 75.3 reduce-scatter.2
  352.1 49.2 all-gather.3
  456.6 56.3 reduce-scatter.4
where the time goes:
time: 690 us; the launch traced here: 689 us
  waiting for transfers between devices  421 us (61%)
  local copies, waits for them, and re-layouts  100 us (14%)
  blocking collectives  58.7 us (9%)
  matrix products  49.5 us (7%)
  starting transfers between devices  22.3 us (3%)
  between operations  21.7 us (3%)
  other arithmetic  14.9 us (2%)
    all_to_all x1, waiting for transfers between devices, on_device(): lax.all_to_all(outgoing, 'tp', split_axis=0, concat_axis=0, tiled=True)  149 us
    reduce_scatter x1, waiting for transfers between devices, on_device(): lax.psum_scatter(jnp.dot(block, w_down, preferred_element_type=jnp.float3...  75.1 us
    psum x1, waiting for transfers between devices, on_device(): lax.psum(up_part.astype(jnp.bfloat16), 'dp').astype(jnp.float32)  71.9 us
    all_gather x1, waiting for transfers between devices, on_device(): pooled = lax.all_gather(received, 'dp', axis=0, tiled=True)  49.3 us
    all_gather x1, waiting for transfers between devices, on_device(): nearby = lax.all_gather(normed[None], 'tp', axis=0, tiled=True)  47.7 us
    unnamed x40, local copies, waits for them, and re-layouts  32.9 us
    all_to_all x1, blocking collectives, on_device(): lax.all_to_all(outgoing_rows, 'tp', split_axis=0, concat_axis=0, tiled=True)  29.9 us
    all_to_all x1, blocking collectives, on_device(): lax.all_to_all(nearby[:, None], 'dp', split_axis=3, concat_axis=1, tiled=...  28.8 us
  transfers between devices with their start and end apart: 8, of which 7 were waited for; matrix products, arithmetic and copies ran while one was open for 3% of the time, Pallas kernels for 0%

commit v1 on v0

--- a/solution.py
+++ b/solution.py
@@ -98,65 +98,50 @@
     context = jnp.concatenate([context_stay, context_moved], axis=0)
     rows_dev = stream.shape[0]
     width = stream.shape[1]
+    both = ("dp", "tp")
+    experts = expert_gate.shape[0] * tp_count
+    shares = gate_scores / jnp.sum(gate_scores, axis=1, keepdims=True) * ROUTE_SCALE
+    hits = expert_ids[:, :, None] == jnp.arange(experts)[None, None, :]
+    spread = jnp.sum(jnp.where(hits, shares[:, :, None], 0.0), axis=1)
+    spread = lax.all_gather(spread, both, axis=0, tiled=True)
+    own_share = lax.dynamic_slice_in_dim(spread, tp_rank, 1, 1)
     normed = rms_scale(stream, dense_gain)
-    nearby = lax.all_gather(normed[None], "tp", axis=0, tiled=True)
-    gathered = lax.all_to_all(nearby[:, None], "dp", split_axis=3, concat_axis=1, tiled=True)
-    features = gathered.reshape(-1, gathered.shape[-1])
+    blocks = lax.all_to_all(
+        normed.reshape(rows_dev, dp_count, -1), "dp", split_axis=1, concat_axis=0, tiled=True
+    )
+    blocks = blocks.reshape(rows_dev * dp_count, -1)
+    features = lax.all_gather(blocks, "tp", axis=0, tiled=True)
     gate_part = jnp.dot(features, w_gate, preferred_element_type=jnp.float32)
     up_part = jnp.dot(features, w_up, preferred_element_type=jnp.float32)
-    gate, up = (
-        lax.psum(gate_part.astype(jnp.bfloat16), "dp").astype(jnp.float32),
-        lax.psum(up_part.astype(jnp.bfloat16), "dp").astype(jnp.float32),
-    )
-    hidden_all = (jax.nn.silu(gate) * up).astype(jnp.bfloat16)
-    block = hidden_all
+    gate = lax.psum_scatter(
+        gate_part.astype(jnp.bfloat16), "dp", scatter_dimension=0, tiled=True
+    ).astype(jnp.float32)
+    up = lax.psum_scatter(
+        up_part.astype(jnp.bfloat16), "dp", scatter_dimension=0, tiled=True
+    ).astype(jnp.float32)
+    hidden = (jax.nn.silu(gate) * up).astype(jnp.bfloat16)
+    hidden_all = lax.all_gather(hidden, "dp", axis=0, tiled=True)
     ffn_share = lax.psum_scatter(
-        jnp.dot(block, w_down, preferred_element_type=jnp.float32).astype(jnp.bfloat16),
+        jnp.dot(hidden_all, w_down, preferred_element_type=jnp.float32).astype(jnp.bfloat16),
         "tp",
         scatter_dimension=0,
         tiled=True,
-    ).astype(jnp.float32)
+    )
     ffn_rows = lax.all_to_all(
-        ffn_share.reshape(dp_count, rows_dev, ffn_share.shape[-1]).astype(jnp.bfloat16),
-        "dp",
-        split_axis=0,
-        concat_axis=2,
-        tiled=True,
+        ffn_share.reshape(dp_count, rows_dev, -1), "dp", split_axis=0, concat_axis=2, tiled=True
     ).astype(jnp.float32)
     middle = (stream.astype(jnp.float32) + ffn_rows[0]).astype(jnp.bfloat16)
     mixed = rms_scale(middle, moe_gain)
-    experts = expert_gate.shape[0] * tp_count
-    top_count = expert_ids.shape[1]
-    capacity = min(rows_dev, rows_dev * top_count // experts + 1)
-    hits = (expert_ids[:, :, None] == jnp.arange(experts)[None, None, :]).astype(jnp.int32)
-    row_hits = jnp.sum(hits, axis=1)
-    before = jnp.cumsum(row_hits, axis=0) - row_hits
-    slot_of = jnp.sum(hits * before[:, None, :], axis=2)
-    target = expert_ids * capacity + slot_of
-    placed = jnp.any(target[:, :, None] == jnp.arange(experts * capacity)[None, None, :], axis=1)
-    outgoing_rows = jnp.dot(
-        placed.T.astype(jnp.bfloat16), mixed, preferred_element_type=jnp.float32
+    pooled = lax.all_gather(mixed, both, axis=0, tiled=True)
+    gate = jnp.dot(pooled, expert_gate[0], preferred_element_type=jnp.float32)
+    up = jnp.dot(pooled, expert_up[0], preferred_element_type=jnp.float32)
+    inner = jnp.where(own_share > 0.0, jax.nn.silu(gate) * up * own_share, 0.0)
+    part = jnp.dot(
+        inner.astype(jnp.bfloat16), expert_down[0], preferred_element_type=jnp.float32
     )
-    outgoing_rows = outgoing_rows.astype(jnp.bfloat16).reshape(experts, capacity, width)
-    received = lax.all_to_all(outgoing_rows, "tp", split_axis=0, concat_axis=0, tiled=True)
-    pooled = lax.all_gather(received, "dp", axis=0, tiled=True)
-    flat = pooled.reshape(-1, width)
-    block = flat
-    gate = jnp.dot(block, expert_gate[0], preferred_element_type=jnp.float32)
-    up = jnp.dot(block, expert_up[0], preferred_element_type=jnp.float32)
-    inner = (jax.nn.silu(gate) * up).astype(jnp.bfloat16)
-    summed = lax.psum_scatter(
-        jnp.dot(inner, expert_down[0], preferred_element_type=jnp.float32).astype(jnp.bfloat16),
-        "dp",
-        scatter_dimension=0,
-        tiled=True,
-    )
-    results = summed.reshape(received.shape)
-    returned = lax.all_to_all(results, "tp", split_axis=0, concat_axis=0, tiled=True)
-    flat_back = returned.reshape(experts * capacity, width)
-    picked = jnp.take(flat_back, target.reshape(-1), axis=0).reshape(rows_dev, top_count, width)
-    shares = gate_scores / jnp.sum(gate_scores, axis=1, keepdims=True) * ROUTE_SCALE
-    routed = jnp.einsum("rk,rkd->rd", shares, picked.astype(jnp.float32))
+    routed = lax.psum_scatter(
+        part.astype(jnp.bfloat16), both, scatter_dimension=0, tiled=True
+    ).astype(jnp.float32)
     stream_out = (middle.astype(jnp.float32) + routed).astype(jnp.bfloat16)
     return (context, arrived, stream_out)
 

time: 690 us -> 1140 us (1.65)
  waiting for transfers between devices: 421 us -> 973 us
  local copies, waits for them, and re-layouts: 100 us -> 8.98 us
  starting transfers between devices: 22.3 us -> 6.5 us
  blocking collectives: 58.7 us -> 72.7 us
    reduce_scatter x2 -> x4, waiting for transfers between devices: 75.1 us -> 762 us  [the longest x1 624 us: on_device(): lax.psum_scatter(part.astype(jnp.bfloat16), both, scatter_dimension=0, ti...]
    psum x1 -> x0, waiting for transfers between devices: 71.9 us -> none  [on_device(): lax.psum(up_part.astype(jnp.bfloat16), 'dp').astype(jnp.float32)]
    all_gather x0 -> x1, blocking collectives: none -> 52.2 us  [on_device(): spread = lax.all_gather(spread, both, axis=0, tiled=True)]
    all_to_all x2, blocking collectives: 58.7 us -> 20.4 us  [the longest x1 10.2 us: on_device(): lax.all_to_all(normed.reshape(rows_dev, dp_count, -1), 'dp', split_axis=1...]
    all_to_all x1, waiting for transfers between devices: 149 us -> 120 us  [on_device(): lax.all_to_all(outgoing, 'tp', split_axis=0, concat_axis=0, tiled=True)]
    all_to_all x2 -> x0, waiting for transfers between devices: 28.6 us -> none  [the longest x1 23 us: on_device(): lax.all_to_all(results, 'tp', split_axis=0, concat_axis=0, tiled=True)]
    unnamed x40 -> x38, local copies, waits for them, and re-layouts: 32.9 us -> 7.26 us
    reshape x5 -> x0, local copies, waits for them, and re-layouts: 18.9 us -> none  [the longest x1 15.1 us: on_device(): flat = pooled.reshape(-1, width)]
  transfers between devices with their start and end apart: 8 -> 8, of which waited for: 7 -> 8; matrix products, arithmetic and copies ran while one was open for 3% -> 2% of each run, Pallas kernels for 0% -> 0%
where the time goes in v1:
time: 1140 us
  waiting for transfers between devices  973 us (85%)
  blocking collectives  72.7 us (6%)
  matrix products  41.6 us (4%)
  between operations  22.1 us (2%)
  other arithmetic  17.7 us (2%)
    reduce_scatter x1, waiting for transfers between devices, on_device(): lax.psum_scatter(part.astype(jnp.bfloat16), both, scatter_dimension=0, ti...  624 us
    all_to_all x1, waiting for transfers between devices, on_device(): lax.all_to_all(outgoing, 'tp', split_axis=0, concat_axis=0, tiled=True)  120 us
    reduce_scatter x1, waiting for transfers between devices, on_device(): lax.psum_scatter(jnp.dot(hidden_all, w_down, preferred_element_type=jnp.f...  75.6 us
    all_gather x1, blocking collectives, on_device(): spread = lax.all_gather(spread, both, axis=0, tiled=True)  52.2 us
    all_gather x1, waiting for transfers between devices, on_device(): features = lax.all_gather(blocks, 'tp', axis=0, tiled=True)  45.2 us
    reduce_scatter x1, waiting for transfers between devices, on_device(): lax.psum_scatter(gate_part.astype(jnp.bfloat16), 'dp', scatter_dimension=...  35.7 us
    reduce_scatter x1, waiting for transfers between devices, on_device(): lax.psum_scatter(up_part.astype(jnp.bfloat16), 'dp', scatter_dimension=0,...  26.4 us
    all_gather x1, waiting for transfers between devices, on_device(): hidden_all = lax.all_gather(hidden, 'dp', axis=0, tiled=True)  24.5 us
  transfers between devices with their start and end apart: 8, of which 8 were waited for; matrix products, arithmetic and copies ran while one was open for 2% of the time, Pallas kernels for 0%

profile of v1, /device:TPU:0, one launch (start us, length us, event | category | flops | bytes accessed | tf_op | source)
XLA Modules:
  0.0 1142.7 jit_solution(7053570754861206711)
XLA Ops:
  7.2 1.2 fusion.39
  8.4 1.0 fusion.41
  9.4 10.2 all_to_all.29
  19.8 45.2 %all-gather.4.cloned.1.call-done = bf16[1024,896]{1,0:T(8,128)(2,1)} async-done(((bf16[64,896]{1,0:T(8,128)(2,1)}), bf16[1024,896]{1,0:T(8,128)(2,1)}) %all-gather.4.cloned.1.call-update) | async-done | bytes 1835024 | tf_op jit(solution)/shard_map/all_gather | solution.py:113
  64.9 5.7 convolution_convert_fusion.1
  70.7 1.5 copy-done.15
  72.3 5.7 convolution_convert_fusion.2
  78.0 26.4 %reduce-scatter.7.cloned.1.call-done = bf16[128,1152]{1,0:T(8,128)(2,1)} async-done(((bf16[1024,1152]{1,0:T(8,128)(2,1)}), bf16[128,1152]{1,0:T(8,128)(2,1)}) %reduce-scatter.7.cloned.1.call-update) | async-done | bytes 294928 | tf_op jit(solution)/shard_map/reduce_scatter | solution.py:119
  104.4 35.7 %reduce-scatter.5.cloned.1.call-done = bf16[128,1152]{1,0:T(8,128)(2,1)} async-done(((bf16[1024,1152]{1,0:T(8,128)(2,1)}), bf16[128,1152]{1,0:T(8,128)(2,1)}) %reduce-scatter.5.cloned.1.call-update) | async-done | bytes 294928 | tf_op jit(solution)/shard_map/reduce_scatter | solution.py:116
  140.1 2.0 fusion.32
  142.1 24.5 %all-gather.6.cloned.1.call-done = bf16[1024,1152]{1,0:T(8,128)(2,1)} async-done(((bf16[128,1152]{1,0:T(8,128)(2,1)}), bf16[1024,1152]{1,0:T(8,128)(2,1)}) %all-gather.6.cloned.1.call-update) | async-done | bytes 2359312 | tf_op jit(solution)/shard_map/all_gather | solution.py:123
  166.6 5.7 convolution_convert_fusion.3
  172.4 75.6 %reduce-scatter.9.cloned.1.call-done = bf16[64,896]{1,0:T(8,128)(2,1)} async-done(((bf16[1024,896]{1,0:T(8,128)(2,1)}), bf16[64,896]{1,0:T(8,128)(2,1)}) %reduce-scatter.9.cloned.1.call-update) | async-done | bytes 114704 | tf_op jit(solution)/shard_map/reduce_scatter | solution.py:124
  248.0 10.2 all_to_all.30
  259.6 52.2 %all_gather.14 = f32[1024,16]{1,0:T(8,128)S(1)} all-gather(f32[8,16]{1,0:T(8,128)S(1)} %select_reduce_fusion), channel_id=1, replica_groups=mesh['dp'=8,'tp'=16] {'dp','tp'}, dimensions={0}, use_global_device_ids=true | all-gather | bytes 66048 | tf_op jit(solution)/shard_map/all_gather | solution.py:106
  312.6 21.5 %all-gather.8.cloned.1.call-done = bf16[1024,7168]{1,0:T(8,128)(2,1)} async-done(((bf16[8,7168]{1,0:T(8,128)(2,1)}), bf16[1024,7168]{1,0:T(8,128)(2,1)}) %all-gather.8.cloned.1.call-update) | async-done | bytes 14680080 | tf_op jit(solution)/shard_map/all_gather | solution.py:135
  334.1 8.8 fusion.3
  342.9 1.6 copy-done.13
  344.5 1.0 copy-done.14
  345.5 4.1 fusion.18
  349.6 7.4 convolution_convert_fusion
  358.3 1.3 iota_compare_fusion.3
  359.7 4.9 select_select_fusion
  364.6 6.2 all-to-all-start
  380.2 1.4 pad_add_fusion
  381.8 2.2 fusion.72
  385.4 119.9 %all-to-all-done = bf16[16,2,256,576]{2,3,1,0:T(8,128)(2,1)} async-done(((bf16[16,2,256,576]{2,3,1,0:T(8,128)(2,1)}), bf16[16,2,256,576]{2,3,1,0:T(8,128)(2,1)}, u32[]{:S(2)}, u32[]{:S(2)}) %all-to-all-start) | async-done | bytes 9437216 | tf_op jit(solution)/shard_map/all_to_all | solution.py:77
  505.3 1.3 dynamic-slice_bitcast_fusion
  506.8 1.1 copy.44
  509.0 1.1 pad_maximum_fusion.1
  510.1 624.2 %reduce-scatter.11.cloned.1.call-done = bf16[8,7168]{1,0:T(8,128)(2,1)} async-done(((bf16[1024,7168]{1,0:T(8,128)(2,1)}), bf16[8,7168]{1,0:T(8,128)(2,1)}) %reduce-scatter.11.cloned.1.call-update) | async-done | bytes 114704 | tf_op jit(solution)/shard_map/reduce_scatter | solution.py:142
  1134.3 1.6 fusion.46
  (87 shorter events, 8.2 us)
Async XLA Ops:
  7.2 57.8 %copy-start = (bf16[896,1152]{1,0:T(8,128)(2,1)S(1)}, bf16[896,1152]{1,0:T(8,128)(2,1)}, u32[]{:S(2)}) copy-start(bf16[896,1152]{1,0:T(8,128)(2,1)} %param.28) | copy-start | bytes 6193156
  7.2 57.8 %all-gather.4.cloned.1.call-start = ((), (), s32[]{:S(2)}) async-start(), calls=%async_computation.7 | async-start | bytes 1949696 | tf_op jit(solution)/shard_map/all_gather | solution.py:113
  19.7 84.7 %reduce-scatter.7.cloned.1.call-start = ((), (), s32[]{:S(2)}) async-start(), calls=%async_computation.9 | async-start | bytes 2654208 | tf_op jit(solution)/shard_map/reduce_scatter | solution.py:119
  70.7 1.6 copy-start.15
  70.7 69.4 %reduce-scatter.5.cloned.1.call-start = ((), (), s32[]{:S(2)}) async-start(), calls=%async_computation.8 | async-start | bytes 2654208 | tf_op jit(solution)/shard_map/reduce_scatter | solution.py:116
  78.0 88.7 %copy-start.16 = (bf16[1152,896]{1,0:T(8,128)(2,1)S(1)}, bf16[1152,896]{1,0:T(8,128)(2,1)}, u32[]{:S(2)}) copy-start(bf16[1152,896]{1,0:T(8,128)(2,1)} %param.29) | copy-start | bytes 6193156
  78.0 88.7 %all-gather.6.cloned.1.call-start = ((), (), s32[]{:S(2)}) async-start(), calls=%async_computation.10 | async-start | bytes 2654208 | tf_op jit(solution)/shard_map/all_gather | solution.py:123
  142.1 106.0 %reduce-scatter.9.cloned.1.call-start = ((), (), s32[]{:S(2)}) async-start(), calls=%async_computation.11 | async-start | bytes 1949696 | tf_op jit(solution)/shard_map/reduce_scatter | solution.py:124
  172.3 85.9 %copy-start.5 = (bf16[8,7168]{1,0:T(8,128)(2,1)S(1)}, bf16[8,7168]{1,0:T(8,128)(2,1)}, u32[]{:S(2)}) copy-start(bf16[8,7168]{1,0:T(8,128)(2,1)} %param.25) | copy-start | bytes 344068
  172.3 86.1 %copy-start.7 = (f32[7168]{0:T(1024)S(1)}, f32[7168]{0:T(1024)}, u32[]{:S(2)}) copy-start(f32[7168]{0:T(1024)} %param.30) | copy-start | bytes 86020
  172.3 87.0 %copy-start.8 = (f32[8,8]{1,0:T(8,128)S(1)}, f32[8,8]{1,0:T(8,128)}, u32[]{:S(2)}) copy-start(f32[8,8]{1,0:T(8,128)} %param.35) | copy-start | bytes 772
  172.3 87.2 %copy-start.9 = (s32[8,8]{1,0:T(8,128)S(1)}, s32[8,8]{1,0:T(8,128)}, u32[]{:S(2)}) copy-start(s32[8,8]{1,0:T(8,128)} %param.34) | copy-start | bytes 772
  172.3 161.7 %all-gather.8.cloned.1.call-start = ((), (), s32[]{:S(2)}) async-start(), calls=%async_computation.12 | async-start | bytes 14794752 | tf_op jit(solution)/shard_map/all_gather | solution.py:135
  259.2 875.1 %reduce-scatter.11.cloned.1.call-start = ((), (), s32[]{:S(2)}) async-start(), calls=%async_computation.13 | async-start | bytes 14794752 | tf_op jit(solution)/shard_map/reduce_scatter | solution.py:142
  334.1 10.4 copy-start.13
  334.1 11.4 %copy-start.14 = (bf16[1,7168,256]{2,1,0:T(8,128)(2,1)S(1)}, bf16[1,7168,256]{2,1,0:T(8,128)(2,1)}, u32[]{:S(2)}) copy-start(bf16[1,7168,256]{2,1,0:T(8,128)(2,1)} %param.32) | copy-start | bytes 11010052
  345.5 4.1 copy-start.3
  357.0 0.7 copy-start.10
  357.0 2.6 copy-start.4
  364.6 15.0 %copy-start.11 = (s32[128,2]{0,1:T(2,128)S(1)}, s32[128,2]{0,1:T(2,128)}, u32[]{:S(2)}) copy-start(s32[128,2]{0,1:T(2,128)} %param.23) | copy-start | bytes 3076
  364.6 17.0 %copy-start.12 = (s32[6]{0:T(128)S(1)}, s32[6]{0:T(128)}, u32[]{:S(2)}) copy-start(s32[6]{0:T(128)} %param.22) | copy-start | bytes 76
  364.6 17.0 %copy-start.6 = (bf16[8,576]{1,0:T(8,128)(2,1)S(1)}, bf16[8,576]{1,0:T(8,128)(2,1)}, u32[]{:S(2)}) copy-start(bf16[8,576]{1,0:T(8,128)(2,1)} %param.19) | copy-start | bytes 27652
  364.6 17.0 %copy-start.2 = (bf16[8,128,576]{1,2,0:T(8,128)(2,1)S(1)}, bf16[8,128,576]{1,2,0:T(8,128)(2,1)}, u32[]{:S(2)}) copy-start(bf16[8,128,576]{1,2,0:T(8,128)(2,1)} %param.18) | copy-start | bytes 3538948
  364.6 140.8 %all-to-all-start = ((bf16[16,2,256,576]{2,3,1,0:T(8,128)(2,1)}), bf16[16,2,256,576]{2,3,1,0:T(8,128)(2,1)}, u32[]{:S(2)}, u32[]{:S(2)}) async-start(bf16[16,2,256,576]{2,3,1,0:T(8,128)(2,1)} %select_select_fusion), calls=%async_computation | async-start | bytes 18874368 | tf_op jit(solution)/shard_map/all_to_all | solution.py:77
  381.8 2.9 copy-start.17
  508.6 627.3 %copy-start.1 = (bf16[896,1152]{1,0:T(8,128)(2,1)S(1)}, bf16[896,1152]{1,0:T(8,128)(2,1)}, u32[]{:S(2)}) copy-start(bf16[896,1152]{1,0:T(8,128)(2,1)} %param.28) | copy-start | bytes 6193156
Sparse Core Ops, SparseCore 0:
  19.8 45.0 all-gather.3
  70.8 33.5 reduce-scatter.6
  106.8 33.1 reduce-scatter.4
  142.2 24.3 all-gather.5
  172.5 75.5 reduce-scatter.8
  259.3 74.6 all-gather.7
  357.2 777.0 reduce-scatter.10

commit v2 on v1

--- a/solution.py
+++ b/solution.py
@@ -1,7 +1,13 @@
+import functools
+
 import jax
 import jax.numpy as jnp
 from jax import lax
+from jax.experimental import pallas as pl
+from jax.experimental.pallas import tpu as pltpu
 from jax.sharding import PartitionSpec as P
+
+MESH = pl.DeviceIdType.MESH
 
 VDIM = 512
 QKD = 192
@@ -39,6 +45,408 @@
         jnp.float32
     )
     return context.astype(jnp.bfloat16)
+
+
+HALF = 3584
+OFFS = (0, 1280, 2432)
+DATA = (1280, 1152, 1152)
+WIDE = (1280, 1280, 1152)
+ORDERS = ((0, 1, 2), (1, 2, 0), (2, 0, 1))
+CUT = 640
+
+
+def place():
+    p, t = lax.axis_index("dp"), lax.axis_index("tp")
+    return [p // 2, t // 4, t % 4], p % 2, p, t
+
+
+def device(at, core):
+    return (at[0] * 2 + core, at[1] * 4 + at[2])
+
+
+def beside(at, axis, step):
+    return [lax.rem(at[a] + 4 + step, 4) if a == axis else at[a] for a in range(3)]
+
+
+class Wires:
+    def __init__(self, send, recv):
+        self.send, self.recv, self.used = send, recv, 0
+        self.open = []
+
+    def start(self, src, dst, peer):
+        i = self.used
+        self.used += 1
+        copy = pltpu.make_async_remote_copy(
+            src_ref=src, dst_ref=dst, send_sem=self.send.at[i], recv_sem=self.recv.at[i],
+            device_id=peer, device_id_type=MESH,
+        )
+        copy.start()
+        self.open.append(copy)
+        return copy
+
+    def close(self):
+        for copy in self.open:
+            copy.wait_send()
+
+
+def greet(peers):
+    barrier = pltpu.get_barrier_semaphore()
+    for peer in peers:
+        pl.semaphore_signal(barrier, inc=1, device_id=peer, device_id_type=MESH)
+    pl.semaphore_wait(barrier, len(peers))
+
+
+def rms(rows, gain):
+    mean_square = jnp.mean(rows * rows, axis=-1, keepdims=True)
+    return (rows * lax.rsqrt(mean_square + EPS) * gain).astype(jnp.bfloat16)
+
+
+def picks(axes_values):
+    return tuple(axes_values)
+
+
+def moe_kernel(
+    middle, gain, ids, scores, eg, eu, ed, out,
+    wgu, wd, acc, inner, swap, swap2, swap3, swap4,
+    ag0, ag1, ag2, ot0, ot1, ot2, po0, po1, po2, pt0, pt1, pt2, pr0, pr1, pr2,
+    ra0, ra1, ra2, rb0, rb1, rb2, rc0, rc1, rc2, rd0, rd1, rd2,
+    q0, q1, q2, qa0, qa1, qa2, qb0, qb1, qb2, qc0, qc1, qc2, qd0, qd1, qd2,
+    s0, s1, s2, sa0, sa1, sa2, sb0, sb1, sb2, sc0, sc1, sc2, sd0, sd1, sd2,
+    load_sem, send_sem, recv_sem, xsend, xrecv,
+):
+    at, core, p, t = place()
+    ag, ot, po, pt, pr = (ag0, ag1, ag2), (ot0, ot1, ot2), (po0, po1, po2), (pt0, pt1, pt2), (pr0, pr1, pr2)
+    loads = [
+        pltpu.make_async_copy(eg, wgu.at[:, 0:256], load_sem.at[0]),
+        pltpu.make_async_copy(eu, wgu.at[:, 256:512], load_sem.at[1]),
+        pltpu.make_async_copy(ed.at[:, 0:HALF], wd.at[0], load_sem.at[2]),
+        pltpu.make_async_copy(ed.at[:, HALF:2 * HALF], wd.at[1], load_sem.at[3]),
+    ]
+    for load in loads:
+        load.start()
+    partner = device(at, 1 - core)
+    greet([partner] + [device(beside(at, a, s), core) for a in range(3) for s in (1, -1)])
+    wires = Wires(send_sem, recv_sem)
+
+    rows = middle[...].astype(jnp.float32)
+    mixed = rms(rows, gain[...]).astype(jnp.float32)
+    given = scores[...]
+    share = given / jnp.sum(given, axis=1, keepdims=True) * ROUTE_SCALE
+    lane = lax.broadcasted_iota(jnp.int32, (8, 128), 1)
+    spread = jnp.zeros((8, 128), jnp.float32)
+    for k in range(8):
+        spread = spread + jnp.where(lane == ids[:, k:k + 1], share[:, k:k + 1], 0.0)
+    high = spread.astype(jnp.bfloat16).astype(jnp.float32)
+    low = (spread - high).astype(jnp.bfloat16).astype(jnp.float32)
+    packed = high + pltpu.roll(low, 16, 1)
+    is_one = core == 1
+    swap[:, 0:HALF] = jnp.where(is_one, mixed[:, 0:HALF], mixed[:, HALF:])
+    swap[:, HALF:] = packed
+    over = wires.start(swap, swap2, partner)
+    mine = jnp.where(is_one, mixed[:, HALF:], mixed[:, 0:HALF])
+    over.wait_recv()
+    theirs = swap2[:, 0:HALF]
+    first = jnp.where(is_one, theirs, mine)
+    second = jnp.where(is_one, mine, theirs)
+    block = jnp.concatenate([first, second], axis=0).astype(jnp.bfloat16)
+    other_pack = swap2[:, HALF:]
+    pack = jnp.concatenate(
+        [jnp.where(is_one, other_pack, packed), jnp.where(is_one, packed, other_pack)], axis=0
+    ).astype(jnp.bfloat16)
+    for k in range(3):
+        ag[k][at[0], at[1], at[2], :, 0:DATA[k]] = block[:, OFFS[k]:OFFS[k] + DATA[k]]
+    ag1[at[0], at[1], at[2], :, DATA[1]:WIDE[1]] = pack
+
+    def spot(k, fixed):
+        return tuple(fixed.get(a, slice(None)) for a in range(3))
+
+    def cols(k, part):
+        return slice(0, CUT) if part == 0 else slice(CUT, WIDE[k])
+
+    def ring(k, axis, fixed):
+        here = spot(k, fixed)
+        up, down = device(beside(at, axis, 1), core), device(beside(at, axis, -1), core)
+        a = wires.start(ag[k].at[here], ag[k].at[here], up)
+        b = wires.start(ag[k].at[here], ag[k].at[here], down)
+        return a, b
+
+    def forward(k, axis, fixed, pair):
+        up, down = device(beside(at, axis, 1), core), device(beside(at, axis, -1), core)
+        below, above = dict(fixed), dict(fixed)
+        below[axis], above[axis] = lax.rem(at[axis] + 3, 4), lax.rem(at[axis] + 1, 4)
+        pair[0].wait_recv()
+        s = spot(k, below) + (slice(None), cols(k, 0))
+        a = wires.start(ag[k].at[s], ag[k].at[s], up)
+        pair[1].wait_recv()
+        s = spot(k, above) + (slice(None), cols(k, 1))
+        b = wires.start(ag[k].at[s], ag[k].at[s], down)
+        return a, b
+
+    own = [{a: at[a] for a in range(3)} for _ in range(3)]
+    pairs = [ring(k, ORDERS[k][0], own[k]) for k in range(3)]
+    pairs = [forward(k, ORDERS[k][0], own[k], pairs[k]) for k in range(3)]
+    second_pairs, third = [None] * 3, [[], [], []]
+    for k in range(3):
+        a1, a2, a3 = ORDERS[k]
+        for c in pairs[k]:
+            c.wait_recv()
+        fixed = {a2: at[a2], a3: at[a3]}
+        second_pairs[k] = ring(k, a2, fixed)
+        third[k].append((fixed, ring(k, a3, fixed)))
+    done2 = [None] * 3
+    for k in range(3):
+        a1, a2, a3 = ORDERS[k]
+        fixed = {a2: at[a2], a3: at[a3]}
+        done2[k] = forward(k, a2, fixed, second_pairs[k])
+        for step in (1, 3):
+            fixed = {a2: lax.rem(at[a2] + step, 4), a3: at[a3]}
+            third[k].append((fixed, ring(k, a3, fixed)))
+    last = [[], [], []]
+    for k in range(3):
+        a1, a2, a3 = ORDERS[k]
+        for c in done2[k]:
+            c.wait_recv()
+        fixed = {a2: lax.rem(at[a2] + 2, 4), a3: at[a3]}
+        third[k].append((fixed, ring(k, a3, fixed)))
+
+    def plane(k, step):
+        return spot(k, {ORDERS[k][2]: lax.rem(at[ORDERS[k][2]] + step, 4)})
+
+    across = [[None] * 4 for _ in range(3)]
+
+    def hand(k, step):
+        s = plane(k, step)
+        across[k][step] = wires.start(ag[k].at[s], ot[k].at[s], partner)
+
+    for k in range(3):
+        hand(k, 0)
+    loads[0].wait()
+    loads[1].wait()
+
+    def product(bufs, half, k, step, fresh):
+        s = plane(k, step)
+        left = bufs[k][s + (slice(None), slice(0, DATA[k]))].reshape(256, DATA[k])
+        base = pl.multiple_of(half * HALF + OFFS[k], 128)
+        part = jnp.dot(left, wgu[pl.ds(base, DATA[k]), :], preferred_element_type=jnp.float32)
+        part = part.reshape(4, 4, 16, 512)
+        acc[s] = acc[s] + part
+
+    acc[...] = jnp.zeros_like(acc)
+    for k in range(3):
+        product(ag, core, k, 0, False)
+    for n in range(4):
+        for k in range(3):
+            fixed, pair = third[k][n]
+            last[k].append(forward(k, ORDERS[k][2], fixed, pair))
+    for k in range(3):
+        hand(k, 1)
+        hand(k, 3)
+
+    def side(n, _):
+        for k in range(3):
+            product(ag, core, k, 2 * n + 1, False)
+        return _
+
+    lax.fori_loop(0, 2, side, 0)
+    for k in range(3):
+        for step in (0, 1, 3):
+            across[k][step].wait_recv()
+
+    def side_other(n, _):
+        for k in range(3):
+            product(ot, 1 - core, k, n + n // 2, False)
+        return _
+
+    lax.fori_loop(0, 3, side_other, 0)
+    for k in range(3):
+        for pair in last[k]:
+            for c in pair:
+                c.wait_recv()
+        hand(k, 2)
+    for k in range(3):
+        product(ag, core, k, 2, False)
+    for k in range(3):
+        across[k][2].wait_recv()
+        product(ot, 1 - core, k, 2, False)
+
+    lane = lax.broadcasted_iota(jnp.int32, (256, 128), 1)
+
+    def activate(n, _):
+        both = acc[n].reshape(256, 512)
+        gate, up = both[:, 0:256], both[:, 256:512]
+        packs = ag1[n, :, :, :, DATA[1]:WIDE[1]].reshape(256, 128).astype(jnp.float32)
+        keep = (lane == t) | (lane == t + 16)
+        weight = jnp.sum(jnp.where(keep, packs, 0.0), axis=1, keepdims=True)
+        value = gate / (1.0 + jnp.exp(-gate)) * up * weight
+        inner[n] = value.astype(jnp.bfloat16).reshape(4, 4, 16, 256)
+        return _
+
+    lax.fori_loop(0, 4, activate, 0)
+    loads[2].wait()
+    loads[3].wait()
+
+    def group(k, step):
+        a1 = ORDERS[k][0]
+        return spot(k, {a1: lax.rem(at[a1] + step, 4)})
+
+    def trade(k, n, step):
+        s = group(k, step)
+        return pltpu.make_async_remote_copy(
+            src_ref=pt[k].at[s], dst_ref=pr[k].at[s], send_sem=xsend.at[k, n], recv_sem=xrecv.at[k, n],
+            device_id=partner, device_id_type=MESH,
+        )
+
+    def step_of(n):
+        return lax.rem(n * 3 + 2, 4) if not isinstance(n, int) else (n * 3 + 2) % 4
+
+    def expand(n, _):
+        for k in range(3):
+            s = group(k, step_of(n))
+            left = inner[s].reshape(256, 256)
+            part = jnp.dot(left, wd[1 - core, :, OFFS[k]:OFFS[k] + DATA[k]], preferred_element_type=jnp.float32)
+            pt[k][s] = part.astype(jnp.bfloat16).reshape(4, 4, 16, DATA[k])
+            trade(k, n, step_of(n)).start()
+            part = jnp.dot(left, wd[core, :, OFFS[k]:OFFS[k] + DATA[k]], preferred_element_type=jnp.float32)
+            po[k][s] = part.astype(jnp.bfloat16).reshape(4, 4, 16, DATA[k])
+        return _
+
+    lax.fori_loop(0, 4, expand, 0)
+
+    ra, rb, rc, rd = (ra0, ra1, ra2), (rb0, rb1, rb2), (rc0, rc1, rc2), (rd0, rd1, rd2)
+
+    def dcols(k, part):
+        return slice(0, CUT) if part == 0 else slice(CUT, DATA[k])
+
+    def meet(k, n):
+        trade(k, n, step_of(n)).wait_recv()
+        s = group(k, step_of(n))
+        po[k][s] = (po[k][s].astype(jnp.float32) + pr[k][s].astype(jnp.float32)).astype(jnp.bfloat16)
+
+    def scatter(bufs, index, axis_of, ra, rb, rc, rd, prepare):
+        state = []
+        for k in range(3):
+            up, down = device(beside(at, axis_of(k), 1), core), device(beside(at, axis_of(k), -1), core)
+            prepare(k, 2)
+            src = index(k, 2)
+            a = wires.start(bufs[k].at[src + (slice(None), dcols(k, 0))], ra[k], down)
+            b = wires.start(bufs[k].at[src + (slice(None), dcols(k, 1))], rb[k], up)
+            state.append([up, down, a, b])
+        for k in range(3):
+            up, down, a, b = state[k]
+            prepare(k, 1)
+            prepare(k, 3)
+            left, right = index(k, 3), index(k, 1)
+            c = wires.start(
+                bufs[k].at[left + (slice(None), dcols(k, 1))], rc[k].at[(slice(None),) * (len(rc[k].shape) - 1) + (dcols(k, 1),)], down
+            )
+            d = wires.start(
+                bufs[k].at[right + (slice(None), dcols(k, 0))], rd[k].at[(slice(None),) * (len(rd[k].shape) - 1) + (dcols(k, 0),)], up
+            )
+            state[k] += [c, d]
+        for k in range(3):
+            up, down, a, b, c, d = state[k]
+            left, right = index(k, 3), index(k, 1)
+            a.wait_recv()
+            s = left + (slice(None), dcols(k, 0))
+            bufs[k][s] = (bufs[k][s].astype(jnp.float32) + ra[k][...].astype(jnp.float32)).astype(jnp.bfloat16)
+            e = wires.start(bufs[k].at[s], rc[k].at[(slice(None),) * (len(rc[k].shape) - 1) + (dcols(k, 0),)], down)
+            b.wait_recv()
+            s = right + (slice(None), dcols(k, 1))
+            bufs[k][s] = (bufs[k][s].astype(jnp.float32) + rb[k][...].astype(jnp.float32)).astype(jnp.bfloat16)
+            f = wires.start(bufs[k].at[s], rd[k].at[(slice(None),) * (len(rd[k].shape) - 1) + (dcols(k, 1),)], up)
+            state[k] += [e, f]
+        sums = []
+        for k in range(3):
+            prepare(k, 0)
+            for c in state[k][4:]:
+                c.wait_recv()
+            yield k, (
+                bufs[k][index(k, 0)].astype(jnp.float32)
+                + rc[k][...].astype(jnp.float32)
+                + rd[k][...].astype(jnp.float32)
+            )
+
+    turn = {2: 0, 1: 1, 3: 3, 0: 2}
+    assert all(step_of(n) == s for s, n in turn.items())
+    q = (q0, q1, q2)
+    for k, total in scatter(
+        po, group, lambda k: ORDERS[k][0], ra, rb, rc, rd, lambda k, step: meet(k, turn[step])
+    ):
+        q[k][...] = total.astype(jnp.bfloat16)
+
+    def group2(k, step):
+        a1, a2, a3 = ORDERS[k]
+        rest = [a for a in range(3) if a != a1]
+        return tuple(lax.rem(at[a] + step, 4) if a == a2 else slice(None) for a in rest)
+
+    s_ = (s0, s1, s2)
+    for k, total in scatter(
+        q, group2, lambda k: ORDERS[k][1], (qa0, qa1, qa2), (qb0, qb1, qb2), (qc0, qc1, qc2), (qd0, qd1, qd2), lambda k, step: None
+    ):
+        s_[k][...] = total.astype(jnp.bfloat16)
+
+    def group3(k, step):
+        return (lax.rem(at[ORDERS[k][2]] + step, 4),)
+
+    for k, total in scatter(
+        s_, group3, lambda k: ORDERS[k][2], (sa0, sa1, sa2), (sb0, sb1, sb2), (sc0, sc1, sc2), (sd0, sd1, sd2), lambda k, step: None
+    ):
+        swap3[:, :, OFFS[k]:OFFS[k] + DATA[k]] = total.reshape(2, 8, DATA[k])
+    over = wires.start(swap3.at[1 - core], swap4, partner)
+    over.wait_recv()
+    lead = jnp.where(is_one, swap4[...], swap3[0])
+    tail = jnp.where(is_one, swap3[1], swap4[...])
+    out[:, 0:HALF] = (rows[:, 0:HALF] + lead).astype(jnp.bfloat16)
+    out[:, HALF:] = (rows[:, HALF:] + tail).astype(jnp.bfloat16)
+    for k in range(3):
+        for n in range(4):
+            trade(k, n, step_of(n)).wait_send()
+    wires.close()
+
+
+def moe(middle, gain, ids, scores, eg, eu, ed):
+    vm, an = pl.BlockSpec(memory_space=pltpu.VMEM), pl.BlockSpec(memory_space=pl.ANY)
+    bf = jnp.bfloat16
+
+    def three(shape, widths):
+        return [pltpu.VMEM(shape + (w,), bf) for w in widths]
+
+    lead, rest = (CUT,) * 3, tuple(w - CUT for w in DATA)
+    cube, face, line, row = (4, 4, 4, 16), (4, 4, 16), (4, 16), (16,)
+    scratch = [
+        pltpu.VMEM((7168, 512), bf),
+        pltpu.VMEM((2, 256, HALF), bf),
+        pltpu.VMEM((4, 4, 4, 16, 512), jnp.float32),
+        pltpu.VMEM((4, 4, 4, 16, 256), bf),
+        pltpu.VMEM((8, HALF + 128), jnp.float32),
+        pltpu.VMEM((8, HALF + 128), jnp.float32),
+        pltpu.VMEM((2, 8, HALF), jnp.float32),
+        pltpu.VMEM((8, HALF), jnp.float32),
+    ]
+    scratch += three(cube, WIDE) + three(cube, WIDE)
+    scratch += three(cube, DATA) + three(cube, DATA) + three(cube, DATA)
+    scratch += three(face, lead) + three(face, rest) + three(face, DATA) + three(face, DATA)
+    for shape in (line, row):
+        big = (4,) + shape
+        scratch += three(big, DATA) + three(shape, lead) + three(shape, rest) + three(shape, DATA) + three(shape, DATA)
+    scratch += [
+        pltpu.SemaphoreType.DMA((4,)),
+        pltpu.SemaphoreType.DMA((160,)),
+        pltpu.SemaphoreType.DMA((160,)),
+        pltpu.SemaphoreType.DMA((3, 4)),
+        pltpu.SemaphoreType.DMA((3, 4)),
+    ]
+    return pl.pallas_call(
+        moe_kernel,
+        out_shape=jax.ShapeDtypeStruct((8, 7168), bf),
+        in_specs=[vm, vm, vm, vm, an, an, an],
+        out_specs=vm,
+        scratch_shapes=scratch,
+        compiler_params=pltpu.CompilerParams(
+            collective_id=1, has_side_effects=True, vmem_limit_bytes=67043328
+        ),
+        name="experts",
+    )(middle, gain, ids, scores, eg, eu, ed)
 
 
 def on_device(
@@ -99,12 +507,6 @@
     rows_dev = stream.shape[0]
     width = stream.shape[1]
     both = ("dp", "tp")
-    experts = expert_gate.shape[0] * tp_count
-    shares = gate_scores / jnp.sum(gate_scores, axis=1, keepdims=True) * ROUTE_SCALE
-    hits = expert_ids[:, :, None] == jnp.arange(experts)[None, None, :]
-    spread = jnp.sum(jnp.where(hits, shares[:, :, None], 0.0), axis=1)
-    spread = lax.all_gather(spread, both, axis=0, tiled=True)
-    own_share = lax.dynamic_slice_in_dim(spread, tp_rank, 1, 1)
     normed = rms_scale(stream, dense_gain)
     blocks = lax.all_to_all(
         normed.reshape(rows_dev, dp_count, -1), "dp", split_axis=1, concat_axis=0, tiled=True
@@ -131,18 +533,9 @@
         ffn_share.reshape(dp_count, rows_dev, -1), "dp", split_axis=0, concat_axis=2, tiled=True
     ).astype(jnp.float32)
     middle = (stream.astype(jnp.float32) + ffn_rows[0]).astype(jnp.bfloat16)
-    mixed = rms_scale(middle, moe_gain)
-    pooled = lax.all_gather(mixed, both, axis=0, tiled=True)
-    gate = jnp.dot(pooled, expert_gate[0], preferred_element_type=jnp.float32)
-    up = jnp.dot(pooled, expert_up[0], preferred_element_type=jnp.float32)
-    inner = jnp.where(own_share > 0.0, jax.nn.silu(gate) * up * own_share, 0.0)
-    part = jnp.dot(
-        inner.astype(jnp.bfloat16), expert_down[0], preferred_element_type=jnp.float32
-    )
-    routed = lax.psum_scatter(
-        part.astype(jnp.bfloat16), both, scatter_dimension=0, tiled=True
-    ).astype(jnp.float32)
-    stream_out = (middle.astype(jnp.float32) + routed).astype(jnp.bfloat16)
+    stream_out = moe(
+        middle, moe_gain[None], expert_ids, gate_scores, expert_gate[0], expert_up[0], expert_down[0]
+    )
     return (context, arrived, stream_out)
 
 

time: 1140 us -> 424 us (0.37)
  waiting for transfers between devices: 973 us -> 231 us
  Pallas kernels: 0 us -> 102 us
  blocking collectives: 72.7 us -> 10.2 us
  matrix products: 41.6 us -> 23.9 us
    reduce_scatter x1 -> x0, waiting for transfers between devices: 624 us -> none  [on_device(): lax.psum_scatter(part.astype(jnp.bfloat16), both, scatter_dimension=0, ti...]
    pallas_call x0 -> x1, Pallas kernels: none -> 102 us  [moe(): pl.pallas_call(moe_kernel, out_shape=jax.ShapeDtypeStruct((8, 7168), bf),...]
    all_to_all x1, waiting for transfers between devices: 120 us -> 66.3 us  [on_device(): lax.all_to_all(outgoing, 'tp', split_axis=0, concat_axis=0, tiled=True)]
    all_gather x1 -> x0, blocking collectives: 52.2 us -> none  [on_device(): spread = lax.all_gather(spread, both, axis=0, tiled=True)]
    reduce_scatter x1, waiting for transfers between devices: 75.6 us -> 51.3 us  [on_device(): lax.psum_scatter(jnp.dot(hidden_all, w_down, preferred_element_type=jnp.f...]
    all_gather x1 -> x0, waiting for transfers between devices: 21.5 us -> none  [on_device(): pooled = lax.all_gather(mixed, both, axis=0, tiled=True)]
    dot_general x3 -> x0, matrix products: 20.3 us -> none  [the longest x1 8.79 us: on_device(): gate = jnp.dot(pooled, expert_gate[0], preferred_element_type=jnp.float32)]
    reduce_scatter x1, waiting for transfers between devices: 26.4 us -> 13.9 us  [on_device(): lax.psum_scatter(up_part.astype(jnp.bfloat16), 'dp', scatter_dimension=0,...]
  transfers between devices with their start and end apart: 8 -> 7, of which waited for: 8 -> 7; matrix products, arithmetic and copies ran while one was open for 2% -> 8% of each run, Pallas kernels for 0% -> 0%
where the time goes in v2:
time: 424 us; the launch traced here: 421 us
  waiting for transfers between devices  231 us (54%)
  Pallas kernels  102 us (24%)
  matrix products  23.9 us (6%)
  between operations  21.6 us (5%)
  other arithmetic  15.2 us (4%)
  blocking collectives  10.2 us (2%)
  starting transfers between devices  9.78 us (2%)
  local copies, waits for them, and re-layouts  7.51 us (2%)
    pallas_call x1, Pallas kernels, moe(): pl.pallas_call(moe_kernel, out_shape=jax.ShapeDtypeStruct((8, 7168), bf),...  102 us
    all_to_all x1, waiting for transfers between devices, on_device(): lax.all_to_all(outgoing, 'tp', split_axis=0, concat_axis=0, tiled=True)  66.3 us
    reduce_scatter x1, waiting for transfers between devices, on_device(): lax.psum_scatter(jnp.dot(hidden_all, w_down, preferred_element_type=jnp.f...  51.3 us
    all_gather x1, waiting for transfers between devices, on_device(): features = lax.all_gather(blocks, 'tp', axis=0, tiled=True)  45.2 us
    reduce_scatter x1, waiting for transfers between devices, on_device(): lax.psum_scatter(gate_part.astype(jnp.bfloat16), 'dp', scatter_dimension=...  36.6 us
    reduce_scatter x1, waiting for transfers between devices, on_device(): lax.psum_scatter(up_part.astype(jnp.bfloat16), 'dp', scatter_dimension=0,...  13.9 us
    all_gather x1, waiting for transfers between devices, on_device(): hidden_all = lax.all_gather(hidden, 'dp', axis=0, tiled=True)  12.5 us
    all_to_all x1, blocking collectives, on_device(): lax.all_to_all(normed.reshape(rows_dev, dp_count, -1), 'dp', split_axis=1...  10.2 us
  transfers between devices with their start and end apart: 7, of which 7 were waited for; matrix products, arithmetic and copies ran while one was open for 8% of the time, Pallas kernels for 0%

profile of v2, /device:TPU:0, one launch (start us, length us, event | category | flops | bytes accessed | tf_op | source)
XLA Modules:
  0.0 421.3 jit_solution(6379806939530700455)
XLA Ops:
  7.2 1.1 fusion.22
  8.3 1.0 fusion.24
  9.3 10.2 %all_to_all.29 = bf16[8,8,896]{2,0,1:T(8,128)(2,1)} all-to-all(bf16[8,8,896]{2,0,1:T(8,128)(2,1)S(1)} %bitcast.75), channel_id=1, replica_groups=mesh['dp'=8,'tp'=16] {'dp'}, dimensions={1} | all-to-all | bytes 229376 | tf_op jit(solution)/shard_map/all_to_all | solution.py:511
  19.6 45.2 %all-gather.3.cloned.1.call-done = bf16[1024,896]{1,0:T(8,128)(2,1)} async-done(((bf16[64,896]{1,0:T(8,128)(2,1)}), bf16[1024,896]{1,0:T(8,128)(2,1)}) %all-gather.3.cloned.1.call-update) | async-done | bytes 1835024 | tf_op jit(solution)/shard_map/all_gather | solution.py:515
  64.8 6.4 %convolution_convert_fusion = bf16[1024,1152]{1,0:T(8,128)(2,1)} fusion(bf16[1024,896]{1,0:T(8,128)(2,1)} %all-gather.3.cloned.1.call-done, bf16[896,1152]{1,0:T(8,128)(2,1)} %param.28), kind=kOutput, calls=%fused_computation.1 | convolution fusion | flops 2115108864 | bytes 6258688 | tf_op jit(solution)/shard_map/dot_general | solution.py:517
  71.2 1.5 copy-done.7
  72.7 5.8 %convolution_convert_fusion.1 = bf16[1024,1152]{1,0:T(8,128)(2,1)} fusion(bf16[1024,896]{1,0:T(8,128)(2,1)} %all-gather.3.cloned.1.call-done, bf16[896,1152]{1,0:T(8,128)(2,1)S(1)} %copy-done.7), kind=kOutput, calls=%fused_computation.2 | convolution fusion | flops 2115108864 | bytes 6258688 | tf_op jit(solution)/shard_map/dot_general | solution.py:516
  78.5 0.7 copy-done.4
  79.2 0.5 fusion.46
  79.8 1.3 iota_compare_fusion.2
  81.2 4.9 %select_select_fusion = bf16[16,2,256,576]{2,3,1,0:T(8,128)(2,1)} fusion(pred[16]{0:T(512)(128)(4,1)S(1)} %get-tuple-element.36, pred[16]{0:T(512)(128)(4,1)S(1)} %get-tuple-element.37, bf16[2,256,576]{1,2,0:T(8,128)(2,1)S(1)} %get-tuple-element.23, bf16[2,256,576]{1,2,0:T(8,128)(2,1)S(1)} %get-tuple-element.22), kind=kLoop, calls=%fused_computation | loop fusion | flops 9437184 | bytes 10616864 | tf_op jit(solution)/shard_map/jit(_where)/select_n | solution.py:482
  86.1 5.1 %all-to-all-start = ((bf16[16,2,256,576]{2,3,1,0:T(8,128)(2,1)}), bf16[16,2,256,576]{2,3,1,0:T(8,128)(2,1)}, u32[]{:S(2)}, u32[]{:S(2)}) async-start(bf16[16,2,256,576]{2,3,1,0:T(8,128)(2,1)} %select_select_fusion), calls=%async_computation | async-start | bytes 18874368 | tf_op jit(solution)/shard_map/all_to_all | solution.py:485
  91.3 13.9 %reduce-scatter.6.cloned.1.call-done = bf16[128,1152]{1,0:T(8,128)(2,1)} async-done(((bf16[1024,1152]{1,0:T(8,128)(2,1)}), bf16[128,1152]{1,0:T(8,128)(2,1)}) %reduce-scatter.6.cloned.1.call-update) | async-done | bytes 294928 | tf_op jit(solution)/shard_map/reduce_scatter | solution.py:521
  105.2 36.6 %reduce-scatter.4.cloned.1.call-done = bf16[128,1152]{1,0:T(8,128)(2,1)} async-done(((bf16[1024,1152]{1,0:T(8,128)(2,1)}), bf16[128,1152]{1,0:T(8,128)(2,1)}) %reduce-scatter.4.cloned.1.call-update) | async-done | bytes 294928 | tf_op jit(solution)/shard_map/reduce_scatter | solution.py:518
  141.8 2.0 fusion.15
  144.4 0.8 select_reduce_fusion.3
  152.8 0.6 fusion.45
  153.7 2.1 fusion.48
  155.9 12.5 %all-gather.5.cloned.1.call-done = bf16[1024,1152]{1,0:T(8,128)(2,1)} async-done(((bf16[128,1152]{1,0:T(8,128)(2,1)}), bf16[1024,1152]{1,0:T(8,128)(2,1)}) %all-gather.5.cloned.1.call-update) | async-done | bytes 2359312 | tf_op jit(solution)/shard_map/all_gather | solution.py:525
  168.4 6.3 %convolution_convert_fusion.2 = bf16[1024,896]{1,0:T(8,128)(2,1)} fusion(bf16[1024,1152]{1,0:T(8,128)(2,1)} %all-gather.5.cloned.1.call-done, bf16[1152,896]{1,0:T(8,128)(2,1)} %param.29), kind=kOutput, calls=%fused_computation.3 | convolution fusion | flops 2114846720 | bytes 6258688 | tf_op jit(solution)/shard_map/dot_general | solution.py:527
  174.7 1.4 pad_add_fusion
  176.7 2.1 add_convert_fusion
  178.8 66.3 %all-to-all-done = bf16[16,2,256,576]{2,3,1,0:T(8,128)(2,1)} async-done(((bf16[16,2,256,576]{2,3,1,0:T(8,128)(2,1)}), bf16[16,2,256,576]{2,3,1,0:T(8,128)(2,1)}, u32[]{:S(2)}, u32[]{:S(2)}) %all-to-all-start) | async-done | bytes 9437216 | tf_op jit(solution)/shard_map/all_to_all | solution.py:485
  245.1 1.3 dynamic-slice_bitcast_fusion
  246.5 1.1 copy.37
  248.8 51.3 %reduce-scatter.8.cloned.1.call-done = bf16[64,896]{1,0:T(8,128)(2,1)} async-done(((bf16[1024,896]{1,0:T(8,128)(2,1)}), bf16[64,896]{1,0:T(8,128)(2,1)}) %reduce-scatter.8.cloned.1.call-update) | async-done | bytes 114704 | tf_op jit(solution)/shard_map/reduce_scatter | solution.py:526
  300.0 4.3 %all-to-all-start.2 = ((bf16[8,8,896]{2,1,0:T(8,128)(2,1)}), bf16[8,8,896]{2,1,0:T(8,128)(2,1)S(1)}, u32[]{:S(2)}, u32[]{:S(2)}) async-start(bf16[8,8,896]{2,1,0:T(8,128)(2,1)} %bitcast.76), calls=%async_computation.5 | async-start | bytes 229376 | tf_op jit(solution)/shard_map/all_to_all | solution.py:532
  304.3 1.1 pad_maximum_fusion.1
  305.4 4.9 %all-to-all-done.2 = bf16[8,8,896]{2,1,0:T(8,128)(2,1)S(1)} async-done(((bf16[8,8,896]{2,1,0:T(8,128)(2,1)}), bf16[8,8,896]{2,1,0:T(8,128)(2,1)S(1)}, u32[]{:S(2)}, u32[]{:S(2)}) %all-to-all-start.2) | async-done | bytes 114720 | tf_op jit(solution)/shard_map/all_to_all | solution.py:532
  310.3 0.7 fusion.25.middle
  310.9 102.2 %experts.1 = bf16[8,7168]{1,0:T(8,128)(2,1)} custom-call(bf16[8,7168]{1,0:T(8,128)(2,1)} %fusion.25.middle, f32[1,7168]{1,0:T(1,128)} %bitcast.77, s32[8,8]{1,0:T(8,128)} %ids.1, f32[8,8]{1,0:T(8,128)} %scores.1, bf16[7168,256]{1,0:T(8,128)(2,1)} %bitcast.70, bf16[7168,256]{1,0:T(8,128)(2,1)} %bitcast.71, bf16[256,7168]{1,0:T(8,128)(2,1)} %bitcast.72), custom_call_target="tpu_custom_call" | custom-call | tf_op jit(solution)/shard_map/experts/pallas_call | solution.py:439
  413.2 1.6 copy.69
  (52 shorter events, 3.2 us)
Async XLA Ops:
  7.2 57.6 %all-gather.3.cloned.1.call-start = ((), (), s32[]{:S(2)}) async-start(), calls=%async_computation.6 | async-start | bytes 1949696 | tf_op jit(solution)/shard_map/all_gather | solution.py:515
  19.6 85.6 %reduce-scatter.6.cloned.1.call-start = ((), (), s32[]{:S(2)}) async-start(), calls=%async_computation.8 | async-start | bytes 2654208 | tf_op jit(solution)/shard_map/reduce_scatter | solution.py:521
  71.1 1.6 copy-start.7
  71.2 70.6 %reduce-scatter.4.cloned.1.call-start = ((), (), s32[]{:S(2)}) async-start(), calls=%async_computation.7 | async-start | bytes 2654208 | tf_op jit(solution)/shard_map/reduce_scatter | solution.py:518
  78.5 0.7 copy-start.4
  78.5 2.6 copy-start.1
  86.1 66.7 %copy-start.5 = (s32[128,2]{0,1:T(2,128)S(1)}, s32[128,2]{0,1:T(2,128)}, u32[]{:S(2)}) copy-start(s32[128,2]{0,1:T(2,128)} %param.23) | copy-start | bytes 3076
  86.1 67.3 %copy-start.6 = (s32[6]{0:T(128)S(1)}, s32[6]{0:T(128)}, u32[]{:S(2)}) copy-start(s32[6]{0:T(128)} %param.22) | copy-start | bytes 76
  86.1 67.4 %copy-start.3 = (bf16[8,576]{1,0:T(8,128)(2,1)S(1)}, bf16[8,576]{1,0:T(8,128)(2,1)}, u32[]{:S(2)}) copy-start(bf16[8,576]{1,0:T(8,128)(2,1)} %param.19) | copy-start | bytes 27652
  86.1 67.4 %copy-start = (bf16[8,128,576]{1,2,0:T(8,128)(2,1)S(1)}, bf16[8,128,576]{1,2,0:T(8,128)(2,1)}, u32[]{:S(2)}) copy-start(bf16[8,128,576]{1,2,0:T(8,128)(2,1)} %param.18) | copy-start | bytes 3538948
  86.1 159.0 %all-to-all-start = ((bf16[16,2,256,576]{2,3,1,0:T(8,128)(2,1)}), bf16[16,2,256,576]{2,3,1,0:T(8,128)(2,1)}, u32[]{:S(2)}, u32[]{:S(2)}) async-start(bf16[16,2,256,576]{2,3,1,0:T(8,128)(2,1)} %select_select_fusion), calls=%async_computation | async-start | bytes 18874368 | tf_op jit(solution)/shard_map/all_to_all | solution.py:485
  91.2 77.1 %all-gather.5.cloned.1.call-start = ((), (), s32[]{:S(2)}) async-start(), calls=%async_computation.9 | async-start | bytes 2654208 | tf_op jit(solution)/shard_map/all_gather | solution.py:525
  143.8 156.3 %reduce-scatter.8.cloned.1.call-start = ((), (), s32[]{:S(2)}) async-start(), calls=%async_computation.10 | async-start | bytes 1949696 | tf_op jit(solution)/shard_map/reduce_scatter | solution.py:526
  248.8 61.5 %copy-start.2 = (bf16[8,7168]{1,0:T(8,128)(2,1)S(1)}, bf16[8,7168]{1,0:T(8,128)(2,1)}, u32[]{:S(2)}) copy-start(bf16[8,7168]{1,0:T(8,128)(2,1)} %param.25) | copy-start | bytes 344068
  300.0 10.2 %all-to-all-start.2 = ((bf16[8,8,896]{2,1,0:T(8,128)(2,1)}), bf16[8,8,896]{2,1,0:T(8,128)(2,1)S(1)}, u32[]{:S(2)}, u32[]{:S(2)}) async-start(bf16[8,8,896]{2,1,0:T(8,128)(2,1)} %bitcast.76), calls=%async_computation.5 | async-start | bytes 229376 | tf_op jit(solution)/shard_map/all_to_all | solution.py:532
Sparse Core Ops, SparseCore 0:
  19.7 45.0 all-gather.2
  71.3 33.8 reduce-scatter.5
  107.6 34.1 reduce-scatter.3
  143.9 24.4 all-gather.4
  174.8 125.1 reduce-scatter.7

commit v3 on v2

--- a/solution.py
+++ b/solution.py
@@ -15,12 +15,6 @@
 
 EPS = 1e-06
 ROUTE_SCALE = 2.5
-
-
-def rms_scale(rows, gain):
-    values = rows.astype(jnp.float32)
-    mean_square = jnp.mean(values * values, axis=-1, keepdims=True)
-    return (values * lax.rsqrt(mean_square + EPS) * gain).astype(jnp.bfloat16)
 
 
 def attend(queries, keys, lengths, newest):
@@ -449,6 +443,465 @@
     )(middle, gain, ids, scores, eg, eu, ed)
 
 
+class Sums:
+    def __init__(self, wires, at, core, axis, buf, index, cut, width, ra, rb, rc, rd):
+        self.wires, self.buf, self.index = wires, buf, index
+        self.up, self.down = device(beside(at, axis, 1), core), device(beside(at, axis, -1), core)
+        self.lead, self.rest = (slice(None), slice(0, cut)), (slice(None), slice(cut, width))
+        self.ra, self.rb, self.rc, self.rd = ra, rb, rc, rd
+
+    def part(self, ref, cols):
+        return ref.at[(slice(None),) * (len(ref.shape) - 2) + cols]
+
+    def far(self):
+        s = self.index(2)
+        self.a = self.wires.start(self.buf.at[s + self.lead], self.ra, self.down)
+        self.b = self.wires.start(self.buf.at[s + self.rest], self.rb, self.up)
+
+    def near(self):
+        left, right = self.index(3), self.index(1)
+        self.c = self.wires.start(self.buf.at[left + self.rest], self.part(self.rc, self.rest), self.down)
+        self.d = self.wires.start(self.buf.at[right + self.lead], self.part(self.rd, self.lead), self.up)
+
+    def add(self, s, other):
+        self.buf[s] = (self.buf[s].astype(jnp.float32) + other[...].astype(jnp.float32)).astype(jnp.bfloat16)
+
+    def relay(self):
+        self.a.wait_recv()
+        s = self.index(3) + self.lead
+        self.add(s, self.ra)
+        self.e = self.wires.start(self.buf.at[s], self.part(self.rc, self.lead), self.down)
+        self.b.wait_recv()
+        s = self.index(1) + self.rest
+        self.add(s, self.rb)
+        self.f = self.wires.start(self.buf.at[s], self.part(self.rd, self.rest), self.up)
+
+    def total(self):
+        for copy in (self.c, self.d, self.e, self.f):
+            copy.wait_recv()
+        return (
+            self.buf[self.index(0)].astype(jnp.float32)
+            + self.rc[...].astype(jnp.float32)
+            + self.rd[...].astype(jnp.float32)
+        )
+
+
+class Spread:
+    def __init__(self, wires, at, core, axis, buf, index, lead, rest):
+        self.wires, self.buf, self.index, self.lead, self.rest = wires, buf, index, lead, rest
+        self.up, self.down = device(beside(at, axis, 1), core), device(beside(at, axis, -1), core)
+
+    def near(self):
+        s = self.index(0)
+        self.a = self.wires.start(self.buf.at[s], self.buf.at[s], self.up)
+        self.b = self.wires.start(self.buf.at[s], self.buf.at[s], self.down)
+
+    def relay(self):
+        self.a.wait_recv()
+        s = self.index(3) + self.lead
+        self.c = self.wires.start(self.buf.at[s], self.buf.at[s], self.up)
+        self.b.wait_recv()
+        s = self.index(1) + self.rest
+        self.d = self.wires.start(self.buf.at[s], self.buf.at[s], self.down)
+
+    def finish(self):
+        self.c.wait_recv()
+        self.d.wait_recv()
+
+
+PLANES = ((1, 2), (2, 1))
+FF = 1152
+FD = 896
+
+
+def dense_kernel(
+    stream, gain, wg, wu, wd, middle,
+    vg, vu, vd, nbuf, land, ft, gu, gx, gra, grb, grc, grd, hid, dn,
+    pa, pb, pc, pd, qs, qa, qb, qc, qd, fin, back,
+    load_sem, send_sem, recv_sem,
+):
+    at, core, p, t = place()
+    loads = [
+        pltpu.make_async_copy(wg, vg, load_sem.at[0]),
+        pltpu.make_async_copy(wu, vu, load_sem.at[1]),
+        pltpu.make_async_copy(wd, vd, load_sem.at[2]),
+    ]
+    for load in loads:
+        load.start()
+    partner = device(at, 1 - core)
+    line = [(lax.rem(p + q, 8), t) for q in range(1, 8)]
+    greet(line + [device(beside(at, a, s), core) for a in (1, 2) for s in (1, -1)])
+    wires = Wires(send_sem, recv_sem)
+
+    rows = stream[...].astype(jnp.float32)
+    normed = rms(rows, gain[...]).astype(jnp.float32)
+    for o in range(8):
+        nbuf[o] = normed[:, o * FD:(o + 1) * FD]
+    sent = [wires.start(nbuf.at[peer[0]], land.at[p], peer) for peer in line]
+    land[p] = nbuf[p]
+
+    for copy in sent:
+        copy.wait_recv()
+    for x in range(4):
+        ft[x // 2, x % 2, at[1], at[2]] = land[2 * x:2 * x + 2].reshape(16, FD).astype(jnp.bfloat16)
+
+    def spots(b, k, fixed):
+        return (b, k) + tuple(fixed.get(a, slice(None)) for a in (1, 2))
+
+    fcut = ((slice(None), slice(0, 512)), (slice(None), slice(512, FD)))
+
+    def spread_of(b, k, axis, other):
+        def index(step):
+            fixed = dict(other)
+            fixed[axis] = lax.rem(at[axis] + step, 4)
+            return spots(b, k, fixed)
+
+        return Spread(wires, at, core, axis, ft, index, *fcut)
+
+    def rem(axis, step):
+        return lax.rem(at[axis] + step, 4)
+
+    first = {(b, k): spread_of(b, k, PLANES[k][0], {PLANES[k][1]: at[PLANES[k][1]]}) for b in (0, 1) for k in (0, 1)}
+    second = {
+        (b, k, j): spread_of(b, k, PLANES[k][1], {PLANES[k][0]: rem(PLANES[k][0], j)})
+        for b in (0, 1) for k in (0, 1) for j in range(4)
+    }
+    for b in (0, 1):
+        for k in (0, 1):
+            first[b, k].near()
+            second[b, k, 0].near()
+    for b in (0, 1):
+        for k in (0, 1):
+            first[b, k].relay()
+            second[b, k, 3].near()
+            second[b, k, 1].near()
+            second[b, k, 0].relay()
+        for k in (0, 1):
+            first[b, k].finish()
+            second[b, k, 2].near()
+    for b in (0, 1):
+        for j in (3, 1, 2):
+            for k in (0, 1):
+                second[b, k, j].relay()
+
+    grows = [(gra.at[b], grb.at[b], grc.at[b], grd.at[b]) for b in (0, 1)]
+    halves = [None, None]
+
+    def project(b):
+        for h in (0, 1):
+            c = (1 - core) if h == 0 else core
+            left = ft[b, c].reshape(256, FD)
+            g = jnp.dot(left, vg[...], preferred_element_type=jnp.float32).astype(jnp.bfloat16)
+            gu[b, c, :, :, 0:FF] = g.reshape(4, 64, FF)
+            u = jnp.dot(left, vu[...], preferred_element_type=jnp.float32).astype(jnp.bfloat16)
+            gu[b, c, :, :, FF:2 * FF] = u.reshape(4, 64, FF)
+            if h == 0:
+                halves[b] = wires.start(gu.at[b, c], gx.at[b], partner)
+
+    def gsum(b):
+        return Sums(
+            wires, at, core, 0, gu, lambda step: (b, core, rem(0, step)), FF, 2 * FF, *grows[b]
+        )
+
+    gsums = [gsum(0), gsum(1)]
+
+    def join(b):
+        halves[b].wait_recv()
+
+        def one(n, _):
+            v = lax.rem(at[0] + n + 2, 4)
+            gu[b, core, v] = (gu[b, core, v].astype(jnp.float32) + gx[b, v].astype(jnp.float32)).astype(jnp.bfloat16)
+            return _
+
+        lax.fori_loop(0, 4, one, 0)
+        gsums[b].far()
+        gsums[b].near()
+
+    hspread = [
+        Spread(wires, at, core, 0, hid, lambda step, b=b: (b, core, rem(0, step)),
+               (slice(None), slice(0, 640)), (slice(None), slice(640, FF)))
+        for b in (0, 1)
+    ]
+    hcross = [[], []]
+
+    def cross(b, step):
+        s = (b, core, rem(0, step))
+        hcross[b].append(wires.start(hid.at[s], hid.at[s], partner))
+
+    def activate(b):
+        both = gsums[b].total()
+        g, u = both[:, 0:FF], both[:, FF:2 * FF]
+        hid[b, core, at[0]] = (g / (1.0 + jnp.exp(-g)) * u).astype(jnp.bfloat16)
+        hspread[b].near()
+        cross(b, 0)
+
+    def hrelay(b):
+        hspread[b].relay()
+        cross(b, 3)
+        cross(b, 1)
+
+    def dsum(b, k):
+        a1, a2 = PLANES[k]
+        return Sums(
+            wires, at, core, a1, dn, lambda step: spots(b, k, {a1: rem(a1, step)}), 512, FD,
+            pa.at[b, k], pb.at[b, k], pc.at[b, k], pd.at[b, k],
+        )
+
+    def dsum2(b, k):
+        a1, a2 = PLANES[k]
+        return Sums(
+            wires, at, core, a2, qs, lambda step: (b, k, rem(a2, step)), 512, FD,
+            qa.at[b, k], qb.at[b, k], qc.at[b, k], qd.at[b, k],
+        )
+
+    ds = {(b, k): dsum(b, k) for b in (0, 1) for k in (0, 1)}
+    ds2 = {(b, k): dsum2(b, k) for b in (0, 1) for k in (0, 1)}
+
+    def contract(b):
+        hspread[b].finish()
+        cross(b, 2)
+        for copy in hcross[b]:
+            copy.wait_recv()
+        for k in (0, 1):
+            left = hid[b, k].reshape(256, FF)
+            part = jnp.dot(left, vd[...], preferred_element_type=jnp.float32)
+            dn[b, k] = part.astype(jnp.bfloat16).reshape(4, 4, 16, FD)
+            ds[b, k].far()
+            ds[b, k].near()
+
+    def drelay(b):
+        for k in (0, 1):
+            ds[b, k].relay()
+
+    def dturn(b):
+        for k in (0, 1):
+            qs[b, k] = ds[b, k].total().astype(jnp.bfloat16)
+            ds2[b, k].far()
+            ds2[b, k].near()
+
+    def dend(b):
+        for k in (0, 1):
+            ds2[b, k].relay()
+        for k in (0, 1):
+            x = 2 * b + k
+            fin[2 * x:2 * x + 2] = ds2[b, k].total().reshape(2, 8, FD)
+
+    for j in range(4):
+        for k in (0, 1):
+            second[0, k, j].finish()
+    loads[0].wait()
+    loads[1].wait()
+    project(0)
+    for j in range(4):
+        for k in (0, 1):
+            second[1, k, j].finish()
+    join(0)
+    project(1)
+    gsums[0].relay()
+    join(1)
+    activate(0)
+    gsums[1].relay()
+    hrelay(0)
+    activate(1)
+    loads[2].wait()
+    contract(0)
+    hrelay(1)
+    contract(1)
+    drelay(0)
+    drelay(1)
+    dturn(0)
+    dturn(1)
+    dend(0)
+    dend(1)
+    sent = [wires.start(fin.at[peer[0]], back.at[p], peer) for peer in line]
+    back[p] = fin[p]
+    for copy in sent:
+        copy.wait_recv()
+    for o in range(8):
+        cols = slice(o * FD, (o + 1) * FD)
+        middle[:, cols] = (rows[:, cols] + back[o]).astype(jnp.bfloat16)
+    wires.close()
+
+
+def dense(stream, gain, wg, wu, wd):
+    vm, an = pl.BlockSpec(memory_space=pltpu.VMEM), pl.BlockSpec(memory_space=pl.ANY)
+    bf, f32 = jnp.bfloat16, jnp.float32
+    scratch = [
+        pltpu.VMEM((FD, FF), bf), pltpu.VMEM((FD, FF), bf), pltpu.VMEM((FF, FD), bf),
+        pltpu.VMEM((8, 8, FD), f32), pltpu.VMEM((8, 8, FD), f32),
+        pltpu.VMEM((2, 2, 4, 4, 16, FD), bf),
+        pltpu.VMEM((2, 2, 4, 64, 2 * FF), bf), pltpu.VMEM((2, 4, 64, 2 * FF), bf),
+        pltpu.VMEM((2, 64, FF), bf), pltpu.VMEM((2, 64, FF), bf),
+        pltpu.VMEM((2, 64, 2 * FF), bf), pltpu.VMEM((2, 64, 2 * FF), bf),
+        pltpu.VMEM((2, 2, 4, 64, FF), bf),
+        pltpu.VMEM((2, 2, 4, 4, 16, FD), bf),
+    ]
+    for lead in ((2, 2, 4, 16), (2, 2, 16)):
+        if len(lead) == 3:
+            scratch.append(pltpu.VMEM((2, 2, 4, 16, FD), bf))
+        scratch += [
+            pltpu.VMEM(lead + (512,), bf), pltpu.VMEM(lead + (FD - 512,), bf),
+            pltpu.VMEM(lead + (FD,), bf), pltpu.VMEM(lead + (FD,), bf),
+        ]
+    scratch += [
+        pltpu.VMEM((8, 8, FD), f32), pltpu.VMEM((8, 8, FD), f32),
+        pltpu.SemaphoreType.DMA((3,)), pltpu.SemaphoreType.DMA((240,)), pltpu.SemaphoreType.DMA((240,)),
+    ]
+    return pl.pallas_call(
+        dense_kernel,
+        out_shape=jax.ShapeDtypeStruct((8, 7168), bf),
+        in_specs=[vm, vm, an, an, an],
+        out_specs=vm,
+        scratch_shapes=scratch,
+        compiler_params=pltpu.CompilerParams(
+            collective_id=2, has_side_effects=True, vmem_limit_bytes=67043328
+        ),
+        name="dense",
+    )(stream, gain, wg, wu, wd)
+
+
+def migrate_kernel(
+    mig, lens, leaving, arrived, got_len,
+    held0, held1, far_out, far_in, near_out, near_in,
+    load_sem, send_sem, recv_sem,
+):
+    at, core, p, t = place()
+    loads = [
+        pltpu.make_async_copy(leaving.at[:, 0], held0.at[at[2]], load_sem.at[0]),
+        pltpu.make_async_copy(leaving.at[:, 1], held1.at[at[1]], load_sem.at[1]),
+    ]
+    for load in loads:
+        load.start()
+    greet([device(beside(at, a, s), core) for a in (1, 2) for s in (1, -1)])
+    wires = Wires(send_sem, recv_sem)
+
+    def rem(axis, step):
+        return lax.rem(at[axis] + step, 4)
+
+    def look(n, state):
+        source, item = n // 2, lax.rem(n, 2)
+        dest = mig[p * 16 + source, item]
+        new = []
+        for i, (count, s0, m0, s1, m1) in enumerate(state):
+            aim = i * 4 + at[2] if i < 4 else at[1] * 4 + (i - 4)
+            hit = dest == aim
+            s0, m0 = jnp.where(hit & (count == 0), source, s0), jnp.where(hit & (count == 0), item, m0)
+            s1, m1 = jnp.where(hit & (count == 1), source, s1), jnp.where(hit & (count == 1), item, m1)
+            new.append((count + jnp.where(hit, 1, 0), s0, m0, s1, m1))
+        return tuple(new)
+
+    zero = jnp.int32(0)
+    table = lax.fori_loop(0, 32, look, ((zero,) * 5,) * 8)
+
+    def choose(values, index):
+        r = values[0]
+        for i in range(1, len(values)):
+            r = jnp.where(index == i, values[i], r)
+        return r
+
+    loads[0].wait()
+    loads[1].wait()
+
+    held = (held0, held1)
+
+    def mover(l):
+        a1 = (2, 1)[l]
+
+        def index(step):
+            return (rem(a1, step),)
+
+        return Spread(wires, at, core, a1, held[l], index, (0,), (1,))
+
+    movers = [mover(0), mover(1)]
+
+    def mine(l, step, slot):
+        a1, a2 = ((2, 1), (1, 2))[l]
+        options = [table[l * 4 + v] for v in range(4)]
+        v = rem(a2, step)
+        source = choose([o[1 + 2 * slot] for o in options], v)
+        item = choose([o[2 + 2 * slot] for o in options], v)
+        y, z = source // 4, lax.rem(source, 4)
+        j, i = (z, y) if l == 0 else (y, z)
+        return i, j, item
+
+    peers2 = [[device(beside(at, a2, 1), core), device(beside(at, a2, -1), core)] for a2 in (1, 2)]
+    far_copies, near_copies = {}, {}
+
+    def merge_far(l):
+        for slot in (0, 1):
+            i, j, item = mine(l, 2, slot)
+            far_out[l, slot] = held[l][j, item]
+            far_copies[l, slot] = wires.start(far_out.at[l, slot], far_in.at[l, slot], peers2[l][1 - slot])
+
+    def merge_near(l, slot, side):
+        step = (3, 1)[side]
+        i, j, item = mine(l, step, slot)
+        if slot == side:
+            far_copies[l, slot].wait_recv()
+            a2 = (1, 2)[l]
+            near_out[l, side, slot] = jnp.where(i == at[a2], held[l][j, item], far_in[l, slot])
+        else:
+            near_out[l, side, slot] = held[l][j, item]
+        near_copies[l, side, slot] = wires.start(
+            near_out.at[l, side, slot], near_in.at[l, side, slot], peers2[l][1 - side]
+        )
+
+    def merge_end(l):
+        a2 = (1, 2)[l]
+        for side in (0, 1):
+            for slot in (0, 1):
+                near_copies[l, side, slot].wait_recv()
+        for slot in (0, 1):
+            i, j, item = mine(l, 0, slot)
+            delta = lax.rem(i - at[a2] + 4, 4)
+            from_above = (delta == 1) | ((delta == 2) if slot == 0 else (delta == 5))
+            other = jnp.where(from_above, near_in[l, 0, slot], near_in[l, 1, slot])
+            arrived[slot, l] = jnp.where(delta == 0, held[l][j, item], other)
+
+    for m in movers:
+        m.near()
+    for m in movers:
+        m.relay()
+    for l, m in enumerate(movers):
+        m.finish()
+        merge_far(l)
+    for l in (0, 1):
+        merge_near(l, 1, 0)
+        merge_near(l, 0, 1)
+    for l in (0, 1):
+        merge_near(l, 0, 0)
+        merge_near(l, 1, 1)
+    for l in (0, 1):
+        merge_end(l)
+    for slot in (0, 1):
+        i, j, item = mine(0, 0, slot)
+        got_len[slot] = lens[p * 16 + i * 4 + j, item]
+    wires.close()
+
+
+def migrate(mig, lens, leaving):
+    vm, an = pl.BlockSpec(memory_space=pltpu.VMEM), pl.BlockSpec(memory_space=pl.ANY)
+    sm = pl.BlockSpec(memory_space=pltpu.SMEM)
+    bf = jnp.bfloat16
+    item = (576, 256)
+    return pl.pallas_call(
+        migrate_kernel,
+        out_shape=(jax.ShapeDtypeStruct((2, 2) + item, bf), jax.ShapeDtypeStruct((2,), jnp.int32)),
+        in_specs=[sm, sm, an],
+        out_specs=(vm, sm),
+        scratch_shapes=[
+            pltpu.VMEM((4, 2) + item, bf), pltpu.VMEM((4, 2) + item, bf),
+            pltpu.VMEM((2, 2) + item, bf), pltpu.VMEM((2, 2) + item, bf),
+            pltpu.VMEM((2, 2, 2) + item, bf), pltpu.VMEM((2, 2, 2) + item, bf),
+            pltpu.SemaphoreType.DMA((2,)), pltpu.SemaphoreType.DMA((24,)), pltpu.SemaphoreType.DMA((24,)),
+        ],
+        compiler_params=pltpu.CompilerParams(
+            collective_id=3, has_side_effects=True, vmem_limit_bytes=67043328
+        ),
+        name="migrate",
+    )(mig, lens, leaving)
+
+
 def on_device(
     queries,
     new_latent,
@@ -469,70 +922,13 @@
     expert_ids,
     gate_scores,
 ):
-    tp_count = lax.axis_size("tp")
-    dp_count = lax.axis_size("dp")
-    tp_rank = lax.axis_index("tp")
-    dp_rank = lax.axis_index("dp")
-    moving = leaving.shape[0]
-    device = dp_rank * tp_count + tp_rank
-    peers = jnp.arange(tp_count)
-    own_dest = lax.dynamic_index_in_dim(mig_dest, device, 0, keepdims=False)
-    outgoing = jnp.zeros((tp_count,) + leaving.shape[1:], jnp.bfloat16)
-    for slot in range(moving):
-        outgoing = jnp.where(
-            (peers == own_dest[slot])[:, None, None, None], leaving[slot][None], outgoing
-        )
-    incoming = lax.all_to_all(outgoing, "tp", split_axis=0, concat_axis=0, tiled=True)
-    group_dest = lax.dynamic_slice_in_dim(mig_dest, dp_rank * tp_count, tp_count, 0)
-    group_len = lax.dynamic_slice_in_dim(leave_len, dp_rank * tp_count, tp_count, 0)
-    match = group_dest == tp_rank
-    is_source = jnp.any(match, axis=1)
-    which = jnp.sum(jnp.where(match, jnp.arange(moving)[None, :], 0), axis=1)
-    order = jnp.cumsum(is_source.astype(jnp.int32)) - 1
-    arrivals = []
-    arrival_len = []
-    for arrival in range(moving):
-        pick = is_source & (order == arrival)
-        source = jnp.sum(jnp.where(pick, peers, 0))
-        slot = jnp.sum(jnp.where(pick, which, 0))
-        arrivals.append(lax.dynamic_index_in_dim(incoming, source, 0, keepdims=False))
-        source_len = lax.dynamic_index_in_dim(group_len, source, 0, keepdims=False)
-        arrival_len.append(lax.dynamic_index_in_dim(source_len, slot, 0, keepdims=False))
-    arrived = jnp.stack(arrivals, axis=0)
-    arrived_len = jnp.stack(arrival_len, axis=0)
+    middle = dense(stream, dense_gain[None], w_gate, w_up, w_down)
+    moved, moved_len = migrate(mig_dest, leave_len, jnp.swapaxes(leaving, 2, 3))
+    arrived = jnp.swapaxes(moved, 2, 3)
     stay = resident.shape[0]
     context_stay = attend(queries[:stay], resident, res_len, new_latent[:stay])
-    context_moved = attend(queries[stay:], arrived[:, 0], arrived_len, new_latent[stay:])
+    context_moved = attend(queries[stay:], arrived[:, 0], moved_len, new_latent[stay:])
     context = jnp.concatenate([context_stay, context_moved], axis=0)
-    rows_dev = stream.shape[0]
-    width = stream.shape[1]
-    both = ("dp", "tp")
-    normed = rms_scale(stream, dense_gain)
-    blocks = lax.all_to_all(
-        normed.reshape(rows_dev, dp_count, -1), "dp", split_axis=1, concat_axis=0, tiled=True
-    )
-    blocks = blocks.reshape(rows_dev * dp_count, -1)
-    features = lax.all_gather(blocks, "tp", axis=0, tiled=True)
-    gate_part = jnp.dot(features, w_gate, preferred_element_type=jnp.float32)
-    up_part = jnp.dot(features, w_up, preferred_element_type=jnp.float32)
-    gate = lax.psum_scatter(
-        gate_part.astype(jnp.bfloat16), "dp", scatter_dimension=0, tiled=True
-    ).astype(jnp.float32)
-    up = lax.psum_scatter(
-        up_part.astype(jnp.bfloat16), "dp", scatter_dimension=0, tiled=True
-    ).astype(jnp.float32)
-    hidden = (jax.nn.silu(gate) * up).astype(jnp.bfloat16)
-    hidden_all = lax.all_gather(hidden, "dp", axis=0, tiled=True)
-    ffn_share = lax.psum_scatter(
-        jnp.dot(hidden_all, w_down, preferred_element_type=jnp.float32).astype(jnp.bfloat16),
-        "tp",
-        scatter_dimension=0,
-        tiled=True,
-    )
-    ffn_rows = lax.all_to_all(
-        ffn_share.reshape(dp_count, rows_dev, -1), "dp", split_axis=0, concat_axis=2, tiled=True
-    ).astype(jnp.float32)
-    middle = (stream.astype(jnp.float32) + ffn_rows[0]).astype(jnp.bfloat16)
     stream_out = moe(
         middle, moe_gain[None], expert_ids, gate_scores, expert_gate[0], expert_up[0], expert_down[0]
     )

time: 424 us -> 267 us (0.63)
  waiting for transfers between devices: 231 us -> 0 us
  Pallas kernels: 102 us -> 249 us
  between operations: 21.6 us -> 0.77 us
  matrix products: 23.9 us -> 4.71 us
  other arithmetic: 15.2 us -> 2.51 us
  blocking collectives: 10.2 us -> 0 us
  starting transfers between devices: 9.78 us -> 0 us
    pallas_call x0 -> x2, Pallas kernels: none -> 146 us  [the longest x1 92.1 us: dense(): pl.pallas_call(dense_kernel, out_shape=jax.ShapeDtypeStruct((8, 7168), bf...]
    reduce_scatter x3 -> x0, waiting for transfers between devices: 102 us -> none  [the longest x1 51.3 us: on_device(): lax.psum_scatter(jnp.dot(hidden_all, w_down, preferred_element_type=jnp.f...]
    all_to_all x2 -> x0, waiting for transfers between devices: 71.1 us -> none  [the longest x1 66.3 us: on_device(): lax.all_to_all(outgoing, 'tp', split_axis=0, concat_axis=0, tiled=True)]
    all_gather x2 -> x0, waiting for transfers between devices: 57.7 us -> none  [the longest x1 45.2 us: on_device(): features = lax.all_gather(blocks, 'tp', axis=0, tiled=True)]
    dot_general x3 -> x0, matrix products: 18.4 us -> none  [the longest x1 6.35 us: on_device(): up_part = jnp.dot(features, w_up, preferred_element_type=jnp.float32)]
    all_to_all x1 -> x0, blocking collectives: 10.2 us -> none  [on_device(): lax.all_to_all(normed.reshape(rows_dev, dp_count, -1), 'dp', split_axis=1...]
    all_to_all x2 -> x0, starting transfers between devices: 9.39 us -> none  [the longest x1 5.13 us: on_device(): lax.all_to_all(outgoing, 'tp', split_axis=0, concat_axis=0, tiled=True)]
    select_n x1 -> x0, other arithmetic: 4.91 us -> none  [on_device(): jnp.where((peers == own_dest[slot])[:, None, None, None], leaving[slot][N...]
  transfers between devices with their start and end apart: 7 -> 0, of which waited for: 7 -> 0; matrix products, arithmetic and copies ran while one was open for 8% -> 0% of each run, Pallas kernels for 0% -> 0%
where the time goes in v3:
time: 267 us; the launch traced here: 265 us
  Pallas kernels  249 us (93%)
  local copies, waits for them, and re-layouts  7.86 us (3%)
  matrix products  4.71 us (2%)
    pallas_call x1, Pallas kernels, moe(): pl.pallas_call(moe_kernel, out_shape=jax.ShapeDtypeStruct((8, 7168), bf),...  103 us
    pallas_call x1, Pallas kernels, dense(): pl.pallas_call(dense_kernel, out_shape=jax.ShapeDtypeStruct((8, 7168), bf...  92.1 us
    pallas_call x1, Pallas kernels, migrate(): pl.pallas_call(migrate_kernel, out_shape=(jax.ShapeDtypeStruct((2, 2) + i...  53.5 us
    unnamed x16, local copies, waits for them, and re-layouts  7.11 us

profile of v3, /device:TPU:0, one launch (start us, length us, event | category | flops | bytes accessed | tf_op | source)
XLA Modules:
  0.0 264.9 jit_solution(579485802906484332)
XLA Ops:
  0.6 1.4 copy.22.mig
  2.0 1.4 copy.23.lens
  3.5 53.5 %migrate.1 = (bf16[2,2,576,256]{3,2,1,0:T(8,128)(2,1)}, s32[2]{0:T(128)}) custom-call(s32[128,2]{1,0:T(8,128)} %copy.22.mig, s32[128,2]{1,0:T(8,128)} %copy.23.lens, bf16[2,2,576,256]{3,2,1,0:T(8,128)(2,1)} %bitcast.48), custom_call_target="tpu_custom_call" | custom-call | tf_op jit(solution)/shard_map/migrate/pallas_call | solution.py:887
  57.0 0.0 copy-start.1
  57.0 0.8 iota_compare_fusion.1
  57.8 0.0 copy-start.3
  57.8 1.6 fusion.33
  59.4 0.7 slice_bitcast_fusion.2
  60.1 1.1 fusion.22
  61.2 0.2 fusion.15
  61.4 0.0 copy-done.1
  61.4 0.0 copy-start.4
  61.4 0.0 copy-start
  61.5 0.0 copy-start.5
  61.5 0.0 copy-done.3
  61.5 0.5 fusion.5
  62.0 0.1 copy-done.4
  62.1 0.1 iota_compare_fusion
  62.2 0.6 copy-done
  62.7 0.6 copy-done.5
  63.3 0.6 fusion.34
  63.9 0.2 fusion.20
  64.2 0.3 fusion.8
  64.5 0.7 add_convert_fusion
  65.2 1.1 pad_maximum_fusion
  66.3 92.1 %dense.1.middle = bf16[8,7168]{1,0:T(8,128)(2,1)} custom-call(bf16[8,7168]{1,0:T(8,128)(2,1)} %stream.1, f32[1,7168]{1,0:T(1,128)} %bitcast.50, bf16[896,1152]{1,0:T(8,128)(2,1)} %wg.1, bf16[896,1152]{1,0:T(8,128)(2,1)} %wu.1, bf16[1152,896]{1,0:T(8,128)(2,1)} %wd.1), custom_call_target="tpu_custom_call" | custom-call | tf_op jit(solution)/shard_map/dense/pallas_call | solution.py:750
  158.4 103.4 %experts.1 = bf16[8,7168]{1,0:T(8,128)(2,1)} custom-call(bf16[8,7168]{1,0:T(8,128)(2,1)} %dense.1.middle, f32[1,7168]{1,0:T(1,128)} %bitcast.49, s32[8,8]{1,0:T(8,128)} %ids.1, f32[8,8]{1,0:T(8,128)} %scores.1, bf16[7168,256]{1,0:T(8,128)(2,1)} %bitcast.42, bf16[7168,256]{1,0:T(8,128)(2,1)} %bitcast.43, bf16[256,7168]{1,0:T(8,128)(2,1)} %bitcast.44), custom_call_target="tpu_custom_call" | custom-call | tf_op jit(solution)/shard_map/experts/pallas_call | solution.py:433
  261.9 0.0 copy-start.2
  261.9 2.4 copy.56
  264.3 0.0 copy-done.2
  264.3 0.6 copy.57
  (8 shorter events, 0.1 us)
Async XLA Ops:
  57.0 4.4 %copy-start.1 = (bf16[2,2,576,256]{3,2,1,0:T(8,128)(2,1)S(1)}, bf16[2,2,576,256]{3,2,1,0:T(8,128)(2,1)}, u32[]{:S(2)}) copy-start(bf16[2,2,576,256]{3,2,1,0:T(8,128)(2,1)} %get-tuple-element.6) | copy-start | bytes 3538948
  57.8 3.7 %copy-start.3 = (bf16[8,576]{1,0:T(8,128)(2,1)S(1)}, bf16[8,576]{1,0:T(8,128)(2,1)}, u32[]{:S(2)}) copy-start(bf16[8,576]{1,0:T(8,128)(2,1)} %param.19) | copy-start | bytes 27652
  61.4 0.7 copy-start.4
  61.4 1.3 copy-start
  61.5 1.8 copy-start.5
  261.9 2.4 copy-start.2

commit v4 on v3

--- a/solution.py
+++ b/solution.py
@@ -515,9 +515,10 @@
 
 
 def dense_kernel(
-    stream, gain, wg, wu, wd, middle,
+    stream, gain, wg, wu, wd, table, leaving, middle, arrived,
     vg, vu, vd, nbuf, land, ft, gu, gx, gra, grb, grc, grd, hid, dn,
     pa, pb, pc, pd, qs, qa, qb, qc, qd, fin, back,
+    held0, held1, far_out, far_in, near_out, near_in,
     load_sem, send_sem, recv_sem,
 ):
     at, core, p, t = place()
@@ -525,6 +526,8 @@
         pltpu.make_async_copy(wg, vg, load_sem.at[0]),
         pltpu.make_async_copy(wu, vu, load_sem.at[1]),
         pltpu.make_async_copy(wd, vd, load_sem.at[2]),
+        pltpu.make_async_copy(leaving.at[:, 0], held0.at[at[2]], load_sem.at[3]),
+        pltpu.make_async_copy(leaving.at[:, 1], held1.at[at[1]], load_sem.at[4]),
     ]
     for load in loads:
         load.start()
@@ -584,6 +587,64 @@
             for k in (0, 1):
                 second[b, k, j].relay()
 
+    loads[3].wait()
+    loads[4].wait()
+
+    held = (held0, held1)
+
+    def mover(l):
+        a1 = (2, 1)[l]
+
+        def index(step):
+            return (rem(a1, step),)
+
+        return Spread(wires, at, core, a1, held[l], index, (0,), (1,))
+
+    movers = [mover(0), mover(1)]
+
+    def mine(l, step, slot):
+        a1, a2 = ((2, 1), (1, 2))[l]
+        row = l * 4 + rem(a2, step)
+        source = table[row, 2 * slot]
+        item = table[row, 2 * slot + 1]
+        y, z = source // 4, lax.rem(source, 4)
+        j, i = (z, y) if l == 0 else (y, z)
+        return i, j, item
+
+    peers2 = [[device(beside(at, a2, 1), core), device(beside(at, a2, -1), core)] for a2 in (1, 2)]
+    far_copies, near_copies = {}, {}
+
+    def merge_far(l):
+        for slot in (0, 1):
+            i, j, item = mine(l, 2, slot)
+            far_out[l, slot] = held[l][j, item]
+            far_copies[l, slot] = wires.start(far_out.at[l, slot], far_in.at[l, slot], peers2[l][1 - slot])
+
+    def merge_near(l, slot, side):
+        step = (3, 1)[side]
+        i, j, item = mine(l, step, slot)
+        if slot == side:
+            far_copies[l, slot].wait_recv()
+            a2 = (1, 2)[l]
+            near_out[l, side, slot] = jnp.where(i == at[a2], held[l][j, item], far_in[l, slot])
+        else:
+            near_out[l, side, slot] = held[l][j, item]
+        near_copies[l, side, slot] = wires.start(
+            near_out.at[l, side, slot], near_in.at[l, side, slot], peers2[l][1 - side]
+        )
+
+    def merge_end(l):
+        a2 = (1, 2)[l]
+        for side in (0, 1):
+            for slot in (0, 1):
+                near_copies[l, side, slot].wait_recv()
+        for slot in (0, 1):
+            i, j, item = mine(l, 0, slot)
+            delta = lax.rem(i - at[a2] + 4, 4)
+            from_above = (delta == 1) | ((delta == 2) if slot == 0 else (delta == 5))
+            other = jnp.where(from_above, near_in[l, 0, slot], near_in[l, 1, slot])
+            arrived[slot, l] = jnp.where(delta == 0, held[l][j, item], other)
+
     grows = [(gra.at[b], grb.at[b], grc.at[b], grd.at[b]) for b in (0, 1)]
     halves = [None, None]
 
@@ -608,12 +669,7 @@
     def join(b):
         halves[b].wait_recv()
 
-        def one(n, _):
-            v = lax.rem(at[0] + n + 2, 4)
-            gu[b, core, v] = (gu[b, core, v].astype(jnp.float32) + gx[b, v].astype(jnp.float32)).astype(jnp.bfloat16)
-            return _
-
-        lax.fori_loop(0, 4, one, 0)
+        gu[b, core] = (gu[b, core].astype(jnp.float32) + gx[b].astype(jnp.float32)).astype(jnp.bfloat16)
         gsums[b].far()
         gsums[b].near()
 
@@ -695,20 +751,36 @@
     for j in range(4):
         for k in (0, 1):
             second[1, k, j].finish()
+    for m in movers:
+        m.near()
     join(0)
     project(1)
     gsums[0].relay()
     join(1)
+    for m in movers:
+        m.relay()
     activate(0)
     gsums[1].relay()
     hrelay(0)
     activate(1)
+    for m in movers:
+        m.finish()
+    for l in (0, 1):
+        merge_far(l)
     loads[2].wait()
+    for l in (0, 1):
+        merge_near(l, 1, 0)
+        merge_near(l, 0, 1)
     contract(0)
     hrelay(1)
+    for l in (0, 1):
+        merge_near(l, 0, 0)
+        merge_near(l, 1, 1)
     contract(1)
     drelay(0)
     drelay(1)
+    for l in (0, 1):
+        merge_end(l)
     dturn(0)
     dturn(1)
     dend(0)
@@ -723,9 +795,11 @@
     wires.close()
 
 
-def dense(stream, gain, wg, wu, wd):
+def dense(stream, gain, wg, wu, wd, table, leaving):
     vm, an = pl.BlockSpec(memory_space=pltpu.VMEM), pl.BlockSpec(memory_space=pl.ANY)
+    sm = pl.BlockSpec(memory_space=pltpu.SMEM)
     bf, f32 = jnp.bfloat16, jnp.float32
+    item = (576, 256)
     scratch = [
         pltpu.VMEM((FD, FF), bf), pltpu.VMEM((FD, FF), bf), pltpu.VMEM((FF, FD), bf),
         pltpu.VMEM((8, 8, FD), f32), pltpu.VMEM((8, 8, FD), f32),
@@ -745,39 +819,29 @@
         ]
     scratch += [
         pltpu.VMEM((8, 8, FD), f32), pltpu.VMEM((8, 8, FD), f32),
-        pltpu.SemaphoreType.DMA((3,)), pltpu.SemaphoreType.DMA((240,)), pltpu.SemaphoreType.DMA((240,)),
+        pltpu.VMEM((4, 2) + item, bf), pltpu.VMEM((4, 2) + item, bf),
+        pltpu.VMEM((2, 2) + item, bf), pltpu.VMEM((2, 2) + item, bf),
+        pltpu.VMEM((2, 2, 2) + item, bf), pltpu.VMEM((2, 2, 2) + item, bf),
+        pltpu.SemaphoreType.DMA((5,)), pltpu.SemaphoreType.DMA((240,)), pltpu.SemaphoreType.DMA((240,)),
     ]
     return pl.pallas_call(
         dense_kernel,
-        out_shape=jax.ShapeDtypeStruct((8, 7168), bf),
-        in_specs=[vm, vm, an, an, an],
-        out_specs=vm,
+        out_shape=(
+            jax.ShapeDtypeStruct((8, 7168), bf),
+            jax.ShapeDtypeStruct((2, 2) + item, bf),
+        ),
+        in_specs=[vm, vm, an, an, an, sm, an],
+        out_specs=(vm, vm),
         scratch_shapes=scratch,
         compiler_params=pltpu.CompilerParams(
             collective_id=2, has_side_effects=True, vmem_limit_bytes=67043328
         ),
         name="dense",
-    )(stream, gain, wg, wu, wd)
-
-
-def migrate_kernel(
-    mig, lens, leaving, arrived, got_len,
-    held0, held1, far_out, far_in, near_out, near_in,
-    load_sem, send_sem, recv_sem,
-):
+    )(stream, gain, wg, wu, wd, table, leaving)
+
+
+def route_kernel(mig, lens, table, got_len):
     at, core, p, t = place()
-    loads = [
-        pltpu.make_async_copy(leaving.at[:, 0], held0.at[at[2]], load_sem.at[0]),
-        pltpu.make_async_copy(leaving.at[:, 1], held1.at[at[1]], load_sem.at[1]),
-    ]
-    for load in loads:
-        load.start()
-    greet([device(beside(at, a, s), core) for a in (1, 2) for s in (1, -1)])
-    wires = Wires(send_sem, recv_sem)
-
-    def rem(axis, step):
-        return lax.rem(at[axis] + step, 4)
-
     def look(n, state):
         source, item = n // 2, lax.rem(n, 2)
         dest = mig[p * 16 + source, item]
@@ -791,115 +855,29 @@
         return tuple(new)
 
     zero = jnp.int32(0)
-    table = lax.fori_loop(0, 32, look, ((zero,) * 5,) * 8)
-
-    def choose(values, index):
-        r = values[0]
-        for i in range(1, len(values)):
-            r = jnp.where(index == i, values[i], r)
-        return r
-
-    loads[0].wait()
-    loads[1].wait()
-
-    held = (held0, held1)
-
-    def mover(l):
-        a1 = (2, 1)[l]
-
-        def index(step):
-            return (rem(a1, step),)
-
-        return Spread(wires, at, core, a1, held[l], index, (0,), (1,))
-
-    movers = [mover(0), mover(1)]
-
-    def mine(l, step, slot):
-        a1, a2 = ((2, 1), (1, 2))[l]
-        options = [table[l * 4 + v] for v in range(4)]
-        v = rem(a2, step)
-        source = choose([o[1 + 2 * slot] for o in options], v)
-        item = choose([o[2 + 2 * slot] for o in options], v)
-        y, z = source // 4, lax.rem(source, 4)
-        j, i = (z, y) if l == 0 else (y, z)
-        return i, j, item
-
-    peers2 = [[device(beside(at, a2, 1), core), device(beside(at, a2, -1), core)] for a2 in (1, 2)]
-    far_copies, near_copies = {}, {}
-
-    def merge_far(l):
-        for slot in (0, 1):
-            i, j, item = mine(l, 2, slot)
-            far_out[l, slot] = held[l][j, item]
-            far_copies[l, slot] = wires.start(far_out.at[l, slot], far_in.at[l, slot], peers2[l][1 - slot])
-
-    def merge_near(l, slot, side):
-        step = (3, 1)[side]
-        i, j, item = mine(l, step, slot)
-        if slot == side:
-            far_copies[l, slot].wait_recv()
-            a2 = (1, 2)[l]
-            near_out[l, side, slot] = jnp.where(i == at[a2], held[l][j, item], far_in[l, slot])
-        else:
-            near_out[l, side, slot] = held[l][j, item]
-        near_copies[l, side, slot] = wires.start(
-            near_out.at[l, side, slot], near_in.at[l, side, slot], peers2[l][1 - side]
-        )
-
-    def merge_end(l):
-        a2 = (1, 2)[l]
-        for side in (0, 1):
-            for slot in (0, 1):
-                near_copies[l, side, slot].wait_recv()
-        for slot in (0, 1):
-            i, j, item = mine(l, 0, slot)
-            delta = lax.rem(i - at[a2] + 4, 4)
-            from_above = (delta == 1) | ((delta == 2) if slot == 0 else (delta == 5))
-            other = jnp.where(from_above, near_in[l, 0, slot], near_in[l, 1, slot])
-            arrived[slot, l] = jnp.where(delta == 0, held[l][j, item], other)
-
-    for m in movers:
-        m.near()
-    for m in movers:
-        m.relay()
-    for l, m in enumerate(movers):
-        m.finish()
-        merge_far(l)
-    for l in (0, 1):
-        merge_near(l, 1, 0)
-        merge_near(l, 0, 1)
-    for l in (0, 1):
-        merge_near(l, 0, 0)
-        merge_near(l, 1, 1)
-    for l in (0, 1):
-        merge_end(l)
+    state = lax.fori_loop(0, 32, look, ((zero,) * 5,) * 8)
+
+    for i in range(8):
+        for n in range(4):
+            table[i, n] = state[i][1 + n]
+    row = at[1]
     for slot in (0, 1):
-        i, j, item = mine(0, 0, slot)
-        got_len[slot] = lens[p * 16 + i * 4 + j, item]
-    wires.close()
-
-
-def migrate(mig, lens, leaving):
-    vm, an = pl.BlockSpec(memory_space=pltpu.VMEM), pl.BlockSpec(memory_space=pl.ANY)
+        source, item = state[0][1 + 2 * slot], state[0][2 + 2 * slot]
+        for i in range(1, 4):
+            source = jnp.where(row == i, state[i][1 + 2 * slot], source)
+            item = jnp.where(row == i, state[i][2 + 2 * slot], item)
+        got_len[slot] = lens[p * 16 + source, item]
+
+
+def route(mig, lens):
     sm = pl.BlockSpec(memory_space=pltpu.SMEM)
-    bf = jnp.bfloat16
-    item = (576, 256)
     return pl.pallas_call(
-        migrate_kernel,
-        out_shape=(jax.ShapeDtypeStruct((2, 2) + item, bf), jax.ShapeDtypeStruct((2,), jnp.int32)),
-        in_specs=[sm, sm, an],
-        out_specs=(vm, sm),
-        scratch_shapes=[
-            pltpu.VMEM((4, 2) + item, bf), pltpu.VMEM((4, 2) + item, bf),
-            pltpu.VMEM((2, 2) + item, bf), pltpu.VMEM((2, 2) + item, bf),
-            pltpu.VMEM((2, 2, 2) + item, bf), pltpu.VMEM((2, 2, 2) + item, bf),
-            pltpu.SemaphoreType.DMA((2,)), pltpu.SemaphoreType.DMA((24,)), pltpu.SemaphoreType.DMA((24,)),
-        ],
-        compiler_params=pltpu.CompilerParams(
-            collective_id=3, has_side_effects=True, vmem_limit_bytes=67043328
-        ),
-        name="migrate",
-    )(mig, lens, leaving)
+        route_kernel,
+        out_shape=(jax.ShapeDtypeStruct((8, 4), jnp.int32), jax.ShapeDtypeStruct((2,), jnp.int32)),
+        in_specs=[sm, sm],
+        out_specs=(sm, sm),
+        name="route",
+    )(mig, lens)
 
 
 def on_device(
@@ -922,8 +900,10 @@
     expert_ids,
     gate_scores,
 ):
-    middle = dense(stream, dense_gain[None], w_gate, w_up, w_down)
-    moved, moved_len = migrate(mig_dest, leave_len, jnp.swapaxes(leaving, 2, 3))
+    table, moved_len = route(mig_dest, leave_len)
+    middle, moved = dense(
+        stream, dense_gain[None], w_gate, w_up, w_down, table, jnp.swapaxes(leaving, 2, 3)
+    )
     arrived = jnp.swapaxes(moved, 2, 3)
     stay = resident.shape[0]
     context_stay = attend(queries[:stay], resident, res_len, new_latent[:stay])

time: 267 us -> 235 us (0.88)
  Pallas kernels: 249 us -> 213 us
  other arithmetic: 2.51 us -> 6.15 us
  matrix products: 4.71 us -> 7.59 us
    pallas_call x2, Pallas kernels: 146 us -> 112 us  [the longest x1 105 us: dense(): pl.pallas_call(dense_kernel, out_shape=(jax.ShapeDtypeStruct((8, 7168), b...]
    unnamed x16 -> x26, local copies, waits for them, and re-layouts: 7.11 us -> 3.77 us
where the time goes in v4:
time: 235 us; the launch traced here: 233 us
  Pallas kernels  213 us (91%)
  matrix products  7.59 us (3%)
  other arithmetic  6.15 us (3%)
  local copies, waits for them, and re-layouts  5.23 us (2%)
    pallas_call x1, Pallas kernels, dense(): pl.pallas_call(dense_kernel, out_shape=(jax.ShapeDtypeStruct((8, 7168), b...  105 us
    pallas_call x1, Pallas kernels, moe(): pl.pallas_call(moe_kernel, out_shape=jax.ShapeDtypeStruct((8, 7168), bf),...  101 us
    pallas_call x1, Pallas kernels, route(): pl.pallas_call(route_kernel, out_shape=(jax.ShapeDtypeStruct((8, 4), jnp....  6.39 us

profile of v4, /device:TPU:0, one launch (start us, length us, event | category | flops | bytes accessed | tf_op | source)
XLA Modules:
  0.0 232.9 jit_solution(534765369403635794)
XLA Ops:
  0.6 0.7 iota_compare_fusion
  1.4 0.7 slice_bitcast_fusion.2
  2.1 1.7 fusion.22
  3.8 1.3 slice_convert_fusion.1
  5.0 0.7 slice_bitcast_fusion.1
  5.8 0.0 copy-start.10
  5.8 1.5 fusion.20
  7.3 0.0 copy-done.4
  7.3 0.0 copy-done.7
  7.3 0.7 copy.23.lens
  8.1 0.7 copy.22.mig
  8.8 6.4 %route.1 = (s32[8,4]{1,0:T(8,128)}, s32[2]{0:T(128)}) custom-call(s32[128,2]{1,0:T(8,128)} %copy.22.mig, s32[128,2]{1,0:T(8,128)} %copy.23.lens), custom_call_target="tpu_custom_call" | custom-call | tf_op jit(solution)/shard_map/route/pallas_call | solution.py:874
  15.2 1.2 iota_compare_fusion.1
  16.5 0.0 copy-done
  16.5 0.6 fusion.34
  17.1 0.3 fusion.8
  17.5 1.6 add_convert_fusion
  19.0 105.3 %dense.1 = (bf16[8,7168]{1,0:T(8,128)(2,1)}, bf16[2,2,576,256]{3,2,1,0:T(8,128)(2,1)}) custom-call(bf16[8,7168]{1,0:T(8,128)(2,1)} %stream.1, f32[1,7168]{1,0:T(1,128)} %bitcast.49, bf16[896,1152]{1,0:T(8,128)(2,1)} %wg.1, bf16[896,1152]{1,0:T(8,128)(2,1)} %wu.1, bf16[1152,896]{1,0:T(8,128)(2,1)} %wd.1, s32[8,4]{1,0:T(8,128)} %get-tuple-element.8.table, ...), custom_call_target="tpu_custom_call" | custom-call | tf_op jit(solution)/shard_map/dense/pallas_call | solution.py:827
  124.4 101.5 %experts.1 = bf16[8,7168]{1,0:T(8,128)(2,1)} custom-call(bf16[8,7168]{1,0:T(8,128)(2,1)} %get-tuple-element.10.middle, f32[1,7168]{1,0:T(1,128)} %bitcast.50, s32[8,8]{1,0:T(8,128)} %ids.1, f32[8,8]{1,0:T(8,128)} %scores.1, bf16[7168,256]{1,0:T(8,128)(2,1)} %bitcast.42, bf16[7168,256]{1,0:T(8,128)(2,1)} %bitcast.43, bf16[256,7168]{1,0:T(8,128)(2,1)} %bitcast.44), custom_call_target="tpu_custom_call" | custom-call | tf_op jit(solution)/shard_map/experts/pallas_call | solution.py:433
  225.9 0.0 copy-start.9
  225.9 1.7 fusion.33
  227.5 0.7 multiply_maximum_fusion
  228.2 0.8 fusion.15
  229.1 0.0 copy-done.1
  229.1 0.0 copy-start.2
  229.1 0.0 copy-done.6
  229.1 0.0 copy-done.9
  229.2 0.5 fusion.5
  229.6 0.6 copy-done.2
  230.2 1.1 pad_maximum_fusion
  231.3 1.0 copy.56
  232.3 0.6 copy.57
  (17 shorter events, 0.1 us)
Async XLA Ops:
  5.7 1.6 copy-start.4
  5.7 1.6 copy-start.7
  5.7 2.3 %copy-start.8 = (s32[128,2]{0,1:T(2,128)S(1)}, s32[128,2]{0,1:T(2,128)}, u32[]{:S(2)}) copy-start(s32[128,2]{0,1:T(2,128)} %param.24) | copy-start | bytes 3076
  5.8 10.7 %copy-start = (bf16[8,128,576]{1,2,0:T(8,128)(2,1)S(1)}, bf16[8,128,576]{1,2,0:T(8,128)(2,1)}, u32[]{:S(2)}) copy-start(bf16[8,128,576]{1,2,0:T(8,128)(2,1)} %param.18) | copy-start | bytes 3538948
  5.8 10.7 %copy-start.10 = (bf16[6,256,576]{1,2,0:T(8,128)(2,1)S(1)}, bf16[6,256,576]{1,2,0:T(8,128)(2,1)}, u32[]{:S(2)}) copy-start(bf16[6,256,576]{1,2,0:T(8,128)(2,1)} %param.20) | copy-start | bytes 5308420
  225.8 3.2 %copy-start.5 = (f32[2,1,128]{2,1,0:T(1,128)S(1)}, f32[2,1,128]{2,1,0:T(1,128)}, u32[]{:S(2)}) copy-start(f32[2,1,128]{2,1,0:T(1,128)} %fusion.22) | copy-start | bytes 3076
  225.8 3.2 %copy-start.1 = (bf16[2,2,576,256]{3,2,1,0:T(8,128)(2,1)S(1)}, bf16[2,2,576,256]{3,2,1,0:T(8,128)(2,1)}, u32[]{:S(2)}) copy-start(bf16[2,2,576,256]{3,2,1,0:T(8,128)(2,1)} %get-tuple-element.9) | copy-start | bytes 3538948
  225.9 3.3 %copy-start.6 = (f32[2,512]{1,0:T(2,128)S(1)}, f32[2,512]{1,0:T(2,128)}, u32[]{:S(2)}) copy-start(f32[2,512]{1,0:T(2,128)} %slice_convert_fusion.1) | copy-start | bytes 12292
  225.9 3.3 %copy-start.9 = (pred[2,256]{1,0:T(4,128)(4,1)S(1)}, pred[2,256]{1,0:T(4,128)(4,1)}, u32[]{:S(2)}) copy-start(pred[2,256]{1,0:T(4,128)(4,1)} %iota_compare_fusion.1) | copy-start | bytes 1540
  229.1 1.1 copy-start.2
  231.3 1.0 copy-start.3

commit v5 on v4

--- a/solution.py
+++ b/solution.py
@@ -105,7 +105,7 @@
     ag0, ag1, ag2, ot0, ot1, ot2, po0, po1, po2, pt0, pt1, pt2, pr0, pr1, pr2,
     ra0, ra1, ra2, rb0, rb1, rb2, rc0, rc1, rc2, rd0, rd1, rd2,
     q0, q1, q2, qa0, qa1, qa2, qb0, qb1, qb2, qc0, qc1, qc2, qd0, qd1, qd2,
-    s0, s1, s2, sa0, sa1, sa2, sb0, sb1, sb2, sc0, sc1, sc2, sd0, sd1, sd2,
+    s0, s1, s2, sx0, sx1, sx2,
     load_sem, send_sem, recv_sem, xsend, xrecv,
 ):
     at, core, p, t = place()
@@ -116,10 +116,8 @@
         pltpu.make_async_copy(ed.at[:, 0:HALF], wd.at[0], load_sem.at[2]),
         pltpu.make_async_copy(ed.at[:, HALF:2 * HALF], wd.at[1], load_sem.at[3]),
     ]
-    for load in loads:
-        load.start()
     partner = device(at, 1 - core)
-    greet([partner] + [device(beside(at, a, s), core) for a in range(3) for s in (1, -1)])
+    greet([partner] + [device(beside(at, a, s), core) for a in range(3) for s in (1, 2, 3)])
     wires = Wires(send_sem, recv_sem)
 
     rows = middle[...].astype(jnp.float32)
@@ -177,8 +175,15 @@
         return a, b
 
     own = [{a: at[a] for a in range(3)} for _ in range(3)]
-    pairs = [ring(k, ORDERS[k][0], own[k]) for k in range(3)]
-    pairs = [forward(k, ORDERS[k][0], own[k], pairs[k]) for k in range(3)]
+    pairs = []
+    for k in range(3):
+        here = spot(k, own[k])
+        pairs.append([
+            wires.start(ag[k].at[here], ag[k].at[here], device(beside(at, ORDERS[k][0], d), core))
+            for d in (2, 1, 3)
+        ])
+    for load in loads:
+        load.start()
     second_pairs, third = [None] * 3, [[], [], []]
     for k in range(3):
         a1, a2, a3 = ORDERS[k]
@@ -252,15 +257,19 @@
         return _
 
     lax.fori_loop(0, 3, side_other, 0)
-    for k in range(3):
-        for pair in last[k]:
-            for c in pair:
+    tails = [[], [], []]
+    for n in range(4):
+        for k in range(3):
+            a2, a3 = ORDERS[k][1:]
+            for c in last[k][n]:
                 c.wait_recv()
-        hand(k, 2)
+            s = spot(k, {a2: third[k][n][0][a2], a3: lax.rem(at[a3] + 2, 4)})
+            tails[k].append(wires.start(ag[k].at[s], ot[k].at[s], partner))
     for k in range(3):
         product(ag, core, k, 2, False)
     for k in range(3):
-        across[k][2].wait_recv()
+        for c in tails[k]:
+            c.wait_recv()
         product(ot, 1 - core, k, 2, False)
 
     lane = lax.broadcasted_iota(jnp.int32, (256, 128), 1)
@@ -304,87 +313,66 @@
             po[k][s] = part.astype(jnp.bfloat16).reshape(4, 4, 16, DATA[k])
         return _
 
-    lax.fori_loop(0, 4, expand, 0)
-
-    ra, rb, rc, rd = (ra0, ra1, ra2), (rb0, rb1, rb2), (rc0, rc1, rc2), (rd0, rd1, rd2)
-
-    def dcols(k, part):
-        return slice(0, CUT) if part == 0 else slice(CUT, DATA[k])
-
     def meet(k, n):
         trade(k, n, step_of(n)).wait_recv()
         s = group(k, step_of(n))
         po[k][s] = (po[k][s].astype(jnp.float32) + pr[k][s].astype(jnp.float32)).astype(jnp.bfloat16)
 
-    def scatter(bufs, index, axis_of, ra, rb, rc, rd, prepare):
-        state = []
-        for k in range(3):
-            up, down = device(beside(at, axis_of(k), 1), core), device(beside(at, axis_of(k), -1), core)
-            prepare(k, 2)
-            src = index(k, 2)
-            a = wires.start(bufs[k].at[src + (slice(None), dcols(k, 0))], ra[k], down)
-            b = wires.start(bufs[k].at[src + (slice(None), dcols(k, 1))], rb[k], up)
-            state.append([up, down, a, b])
-        for k in range(3):
-            up, down, a, b = state[k]
-            prepare(k, 1)
-            prepare(k, 3)
-            left, right = index(k, 3), index(k, 1)
-            c = wires.start(
-                bufs[k].at[left + (slice(None), dcols(k, 1))], rc[k].at[(slice(None),) * (len(rc[k].shape) - 1) + (dcols(k, 1),)], down
-            )
-            d = wires.start(
-                bufs[k].at[right + (slice(None), dcols(k, 0))], rd[k].at[(slice(None),) * (len(rd[k].shape) - 1) + (dcols(k, 0),)], up
-            )
-            state[k] += [c, d]
-        for k in range(3):
-            up, down, a, b, c, d = state[k]
-            left, right = index(k, 3), index(k, 1)
-            a.wait_recv()
-            s = left + (slice(None), dcols(k, 0))
-            bufs[k][s] = (bufs[k][s].astype(jnp.float32) + ra[k][...].astype(jnp.float32)).astype(jnp.bfloat16)
-            e = wires.start(bufs[k].at[s], rc[k].at[(slice(None),) * (len(rc[k].shape) - 1) + (dcols(k, 0),)], down)
-            b.wait_recv()
-            s = right + (slice(None), dcols(k, 1))
-            bufs[k][s] = (bufs[k][s].astype(jnp.float32) + rb[k][...].astype(jnp.float32)).astype(jnp.bfloat16)
-            f = wires.start(bufs[k].at[s], rd[k].at[(slice(None),) * (len(rd[k].shape) - 1) + (dcols(k, 1),)], up)
-            state[k] += [e, f]
-        sums = []
-        for k in range(3):
-            prepare(k, 0)
-            for c in state[k][4:]:
-                c.wait_recv()
-            yield k, (
-                bufs[k][index(k, 0)].astype(jnp.float32)
-                + rc[k][...].astype(jnp.float32)
-                + rd[k][...].astype(jnp.float32)
-            )
-
-    turn = {2: 0, 1: 1, 3: 3, 0: 2}
-    assert all(step_of(n) == s for s, n in turn.items())
+    sums = [
+        Sums(
+            wires, at, core, ORDERS[k][0], po[k], lambda step, k=k: group(k, step), CUT, DATA[k],
+            (ra0, ra1, ra2)[k], (rb0, rb1, rb2)[k], (rc0, rc1, rc2)[k], (rd0, rd1, rd2)[k],
+        )
+        for k in range(3)
+    ]
+    lax.fori_loop(0, 2, expand, 0)
+    for k in range(3):
+        meet(k, 0)
+        sums[k].far()
+    lax.fori_loop(2, 4, expand, 0)
+    for k in range(3):
+        meet(k, 1)
+        meet(k, 3)
+        sums[k].near()
+    for k in range(3):
+        sums[k].relay()
+    for k in range(3):
+        meet(k, 2)
     q = (q0, q1, q2)
-    for k, total in scatter(
-        po, group, lambda k: ORDERS[k][0], ra, rb, rc, rd, lambda k, step: meet(k, turn[step])
-    ):
-        q[k][...] = total.astype(jnp.bfloat16)
 
     def group2(k, step):
         a1, a2, a3 = ORDERS[k]
         rest = [a for a in range(3) if a != a1]
         return tuple(lax.rem(at[a] + step, 4) if a == a2 else slice(None) for a in rest)
 
-    s_ = (s0, s1, s2)
-    for k, total in scatter(
-        q, group2, lambda k: ORDERS[k][1], (qa0, qa1, qa2), (qb0, qb1, qb2), (qc0, qc1, qc2), (qd0, qd1, qd2), lambda k, step: None
-    ):
-        s_[k][...] = total.astype(jnp.bfloat16)
-
-    def group3(k, step):
-        return (lax.rem(at[ORDERS[k][2]] + step, 4),)
-
-    for k, total in scatter(
-        s_, group3, lambda k: ORDERS[k][2], (sa0, sa1, sa2), (sb0, sb1, sb2), (sc0, sc1, sc2), (sd0, sd1, sd2), lambda k, step: None
-    ):
+    sums2 = [
+        Sums(
+            wires, at, core, ORDERS[k][1], q[k], lambda step, k=k: group2(k, step), CUT, DATA[k],
+            (qa0, qa1, qa2)[k], (qb0, qb1, qb2)[k], (qc0, qc1, qc2)[k], (qd0, qd1, qd2)[k],
+        )
+        for k in range(3)
+    ]
+    for k in range(3):
+        q[k][...] = sums[k].total().astype(jnp.bfloat16)
+        sums2[k].far()
+        sums2[k].near()
+    for k in range(3):
+        sums2[k].relay()
+    s_, sx = (s0, s1, s2), (sx0, sx1, sx2)
+    final = []
+    for k in range(3):
+        s_[k][...] = sums2[k].total().astype(jnp.bfloat16)
+        a3 = ORDERS[k][2]
+        final.append([
+            wires.start(s_[k].at[lax.rem(at[a3] + d, 4)], sx[k].at[d - 1], device(beside(at, a3, d), core))
+            for d in (2, 1, 3)
+        ])
+    for k in range(3):
+        for copy in final[k]:
+            copy.wait_recv()
+        total = s_[k][at[ORDERS[k][2]]].astype(jnp.float32)
+        for d in range(3):
+            total = total + sx[k][d].astype(jnp.float32)
         swap3[:, :, OFFS[k]:OFFS[k] + DATA[k]] = total.reshape(2, 8, DATA[k])
     over = wires.start(swap3.at[1 - core], swap4, partner)
     over.wait_recv()
@@ -420,9 +408,9 @@
     scratch += three(cube, WIDE) + three(cube, WIDE)
     scratch += three(cube, DATA) + three(cube, DATA) + three(cube, DATA)
     scratch += three(face, lead) + three(face, rest) + three(face, DATA) + three(face, DATA)
-    for shape in (line, row):
-        big = (4,) + shape
-        scratch += three(big, DATA) + three(shape, lead) + three(shape, rest) + three(shape, DATA) + three(shape, DATA)
+    scratch += three((4,) + line, DATA)
+    scratch += three(line, lead) + three(line, rest) + three(line, DATA) + three(line, DATA)
+    scratch += three((4,) + row, DATA) + three((3,) + row, DATA)
     scratch += [
         pltpu.SemaphoreType.DMA((4,)),
         pltpu.SemaphoreType.DMA((160,)),
@@ -517,7 +505,7 @@
 def dense_kernel(
     stream, gain, wg, wu, wd, table, leaving, middle, arrived,
     vg, vu, vd, nbuf, land, ft, gu, gx, gra, grb, grc, grd, hid, dn,
-    pa, pb, pc, pd, qs, qa, qb, qc, qd, fin, back,
+    pa, pb, pc, pd, qs, qx, fin, back,
     held0, held1, far_out, far_in, near_out, near_in,
     load_sem, send_sem, recv_sem,
 ):
@@ -529,11 +517,9 @@
         pltpu.make_async_copy(leaving.at[:, 0], held0.at[at[2]], load_sem.at[3]),
         pltpu.make_async_copy(leaving.at[:, 1], held1.at[at[1]], load_sem.at[4]),
     ]
-    for load in loads:
-        load.start()
     partner = device(at, 1 - core)
     line = [(lax.rem(p + q, 8), t) for q in range(1, 8)]
-    greet(line + [device(beside(at, a, s), core) for a in (1, 2) for s in (1, -1)])
+    greet(line + [device(beside(at, a, s), core) for a in (1, 2) for s in (1, 2, 3)])
     wires = Wires(send_sem, recv_sem)
 
     rows = stream[...].astype(jnp.float32)
@@ -541,6 +527,8 @@
     for o in range(8):
         nbuf[o] = normed[:, o * FD:(o + 1) * FD]
     sent = [wires.start(nbuf.at[peer[0]], land.at[p], peer) for peer in line]
+    for load in loads:
+        load.start()
     land[p] = nbuf[p]
 
     for copy in sent:
@@ -564,24 +552,28 @@
     def rem(axis, step):
         return lax.rem(at[axis] + step, 4)
 
-    first = {(b, k): spread_of(b, k, PLANES[k][0], {PLANES[k][1]: at[PLANES[k][1]]}) for b in (0, 1) for k in (0, 1)}
+    first = {}
     second = {
         (b, k, j): spread_of(b, k, PLANES[k][1], {PLANES[k][0]: rem(PLANES[k][0], j)})
         for b in (0, 1) for k in (0, 1) for j in range(4)
     }
     for b in (0, 1):
         for k in (0, 1):
-            first[b, k].near()
+            here = (b, k, at[1], at[2])
+            first[b, k] = [
+                wires.start(ft.at[here], ft.at[here], device(beside(at, PLANES[k][0], d), core)) for d in (1, 3, 2)
+            ]
             second[b, k, 0].near()
     for b in (0, 1):
         for k in (0, 1):
-            first[b, k].relay()
+            first[b, k][0].wait_recv()
             second[b, k, 3].near()
+            first[b, k][1].wait_recv()
             second[b, k, 1].near()
+            first[b, k][2].wait_recv()
+            second[b, k, 2].near()
+        for k in (0, 1):
             second[b, k, 0].relay()
-        for k in (0, 1):
-            first[b, k].finish()
-            second[b, k, 2].near()
     for b in (0, 1):
         for j in (3, 1, 2):
             for k in (0, 1):
@@ -605,8 +597,8 @@
     def mine(l, step, slot):
         a1, a2 = ((2, 1), (1, 2))[l]
         row = l * 4 + rem(a2, step)
-        source = table[row, 2 * slot]
-        item = table[row, 2 * slot + 1]
+        pick = table[row, slot]
+        source, item = pick // 2, lax.rem(pick, 2)
         y, z = source // 4, lax.rem(source, 4)
         j, i = (z, y) if l == 0 else (y, z)
         return i, j, item
@@ -703,15 +695,8 @@
             pa.at[b, k], pb.at[b, k], pc.at[b, k], pd.at[b, k],
         )
 
-    def dsum2(b, k):
-        a1, a2 = PLANES[k]
-        return Sums(
-            wires, at, core, a2, qs, lambda step: (b, k, rem(a2, step)), 512, FD,
-            qa.at[b, k], qb.at[b, k], qc.at[b, k], qd.at[b, k],
-        )
-
     ds = {(b, k): dsum(b, k) for b in (0, 1) for k in (0, 1)}
-    ds2 = {(b, k): dsum2(b, k) for b in (0, 1) for k in (0, 1)}
+    ds2 = {}
 
     def contract(b):
         hspread[b].finish()
@@ -732,15 +717,21 @@
     def dturn(b):
         for k in (0, 1):
             qs[b, k] = ds[b, k].total().astype(jnp.bfloat16)
-            ds2[b, k].far()
-            ds2[b, k].near()
+            a2 = PLANES[k][1]
+            ds2[b, k] = [
+                wires.start(qs.at[b, k, rem(a2, d)], qx.at[b, k, d - 1], device(beside(at, a2, d), core))
+                for d in (2, 1, 3)
+            ]
 
     def dend(b):
         for k in (0, 1):
-            ds2[b, k].relay()
-        for k in (0, 1):
             x = 2 * b + k
-            fin[2 * x:2 * x + 2] = ds2[b, k].total().reshape(2, 8, FD)
+            for copy in ds2[b, k]:
+                copy.wait_recv()
+            total = qs[b, k, at[PLANES[k][1]]].astype(jnp.float32)
+            for d in range(3):
+                total = total + qx[b, k, d].astype(jnp.float32)
+            fin[2 * x:2 * x + 2] = total.reshape(2, 8, FD)
 
     for j in range(4):
         for k in (0, 1):
@@ -753,29 +744,29 @@
             second[1, k, j].finish()
     for m in movers:
         m.near()
+    project(1)
     join(0)
-    project(1)
+    join(1)
     gsums[0].relay()
-    join(1)
     for m in movers:
         m.relay()
+    gsums[1].relay()
     activate(0)
-    gsums[1].relay()
-    hrelay(0)
-    activate(1)
     for m in movers:
         m.finish()
     for l in (0, 1):
         merge_far(l)
-    loads[2].wait()
     for l in (0, 1):
         merge_near(l, 1, 0)
         merge_near(l, 0, 1)
-    contract(0)
-    hrelay(1)
+    activate(1)
+    hrelay(0)
     for l in (0, 1):
         merge_near(l, 0, 0)
         merge_near(l, 1, 1)
+    hrelay(1)
+    loads[2].wait()
+    contract(0)
     contract(1)
     drelay(0)
     drelay(1)
@@ -810,14 +801,11 @@
         pltpu.VMEM((2, 2, 4, 64, FF), bf),
         pltpu.VMEM((2, 2, 4, 4, 16, FD), bf),
     ]
-    for lead in ((2, 2, 4, 16), (2, 2, 16)):
-        if len(lead) == 3:
-            scratch.append(pltpu.VMEM((2, 2, 4, 16, FD), bf))
-        scratch += [
-            pltpu.VMEM(lead + (512,), bf), pltpu.VMEM(lead + (FD - 512,), bf),
-            pltpu.VMEM(lead + (FD,), bf), pltpu.VMEM(lead + (FD,), bf),
-        ]
+    lead = (2, 2, 4, 16)
     scratch += [
+        pltpu.VMEM(lead + (512,), bf), pltpu.VMEM(lead + (FD - 512,), bf),
+        pltpu.VMEM(lead + (FD,), bf), pltpu.VMEM(lead + (FD,), bf),
+        pltpu.VMEM((2, 2, 4, 16, FD), bf), pltpu.VMEM((2, 2, 3, 16, FD), bf),
         pltpu.VMEM((8, 8, FD), f32), pltpu.VMEM((8, 8, FD), f32),
         pltpu.VMEM((4, 2) + item, bf), pltpu.VMEM((4, 2) + item, bf),
         pltpu.VMEM((2, 2) + item, bf), pltpu.VMEM((2, 2) + item, bf),
@@ -840,44 +828,19 @@
     )(stream, gain, wg, wu, wd, table, leaving)
 
 
-def route_kernel(mig, lens, table, got_len):
-    at, core, p, t = place()
-    def look(n, state):
-        source, item = n // 2, lax.rem(n, 2)
-        dest = mig[p * 16 + source, item]
-        new = []
-        for i, (count, s0, m0, s1, m1) in enumerate(state):
-            aim = i * 4 + at[2] if i < 4 else at[1] * 4 + (i - 4)
-            hit = dest == aim
-            s0, m0 = jnp.where(hit & (count == 0), source, s0), jnp.where(hit & (count == 0), item, m0)
-            s1, m1 = jnp.where(hit & (count == 1), source, s1), jnp.where(hit & (count == 1), item, m1)
-            new.append((count + jnp.where(hit, 1, 0), s0, m0, s1, m1))
-        return tuple(new)
-
-    zero = jnp.int32(0)
-    state = lax.fori_loop(0, 32, look, ((zero,) * 5,) * 8)
-
-    for i in range(8):
-        for n in range(4):
-            table[i, n] = state[i][1 + n]
-    row = at[1]
-    for slot in (0, 1):
-        source, item = state[0][1 + 2 * slot], state[0][2 + 2 * slot]
-        for i in range(1, 4):
-            source = jnp.where(row == i, state[i][1 + 2 * slot], source)
-            item = jnp.where(row == i, state[i][2 + 2 * slot], item)
-        got_len[slot] = lens[p * 16 + source, item]
-
-
-def route(mig, lens):
-    sm = pl.BlockSpec(memory_space=pltpu.SMEM)
-    return pl.pallas_call(
-        route_kernel,
-        out_shape=(jax.ShapeDtypeStruct((8, 4), jnp.int32), jax.ShapeDtypeStruct((2,), jnp.int32)),
-        in_specs=[sm, sm],
-        out_specs=(sm, sm),
-        name="route",
-    )(mig, lens)
+def route(mig_dest, leave_len):
+    p, t = lax.axis_index("dp"), lax.axis_index("tp")
+    group = lax.dynamic_slice_in_dim(mig_dest, p * 16, 16, 0).reshape(1, 32)
+    lens = lax.dynamic_slice_in_dim(leave_len, p * 16, 16, 0).reshape(1, 32)
+    step = jnp.arange(4)
+    aims = jnp.concatenate([step * 4 + t % 4, t // 4 * 4 + step, t[None]])[:, None]
+    hit = group == aims
+    order = jnp.arange(32)[None, :]
+    low = jnp.min(jnp.where(hit, order, 32), axis=1)
+    high = jnp.max(jnp.where(hit, order, -1), axis=1)
+    ends = jnp.stack([low, high], axis=1)
+    got = jnp.sum(jnp.where(order == ends[8][:, None], lens, 0), axis=1)
+    return ends, got
 
 
 def on_device(

time: 235 us -> 208 us (0.89)
  Pallas kernels: 213 us -> 186 us
    pallas_call x1, Pallas kernels: 105 us -> 92.5 us  [dense(): pl.pallas_call(dense_kernel, out_shape=(jax.ShapeDtypeStruct((8, 7168), b...]
    pallas_call x1, Pallas kernels: 101 us -> 93.2 us  [moe(): pl.pallas_call(moe_kernel, out_shape=jax.ShapeDtypeStruct((8, 7168), bf),...]
    pallas_call x1 -> x0, Pallas kernels: 6.39 us -> none  [route(): pl.pallas_call(route_kernel, out_shape=(jax.ShapeDtypeStruct((8, 4), jnp....]
where the time goes in v5:
time: 208 us; the launch traced here: 206 us
  Pallas kernels  186 us (89%)
  matrix products  7.58 us (4%)
  local copies, waits for them, and re-layouts  6.26 us (3%)
  other arithmetic  6.07 us (3%)
    pallas_call x1, Pallas kernels, moe(): pl.pallas_call(moe_kernel, out_shape=jax.ShapeDtypeStruct((8, 7168), bf),...  93.2 us
    pallas_call x1, Pallas kernels, dense(): pl.pallas_call(dense_kernel, out_shape=(jax.ShapeDtypeStruct((8, 7168), b...  92.5 us

profile of v5, /device:TPU:0, one launch (start us, length us, event | category | flops | bytes accessed | tf_op | source)
XLA Modules:
  0.0 206.4 jit_solution(12195870985176566855)
XLA Ops:
  0.7 0.1 pad_add_fusion.1
  0.7 0.8 constant_dynamic-slice_fusion
  1.5 0.7 iota_compare_fusion
  2.2 0.7 slice_bitcast_fusion.2
  3.0 1.7 fusion.24
  4.7 1.3 slice_convert_fusion.1
  5.9 0.1 copy.49
  6.0 0.1 broadcast_in_dim.103
  6.1 0.1 copy.48
  6.2 0.1 eq.33
  6.3 0.2 fusion.22
  6.5 0.2 slice_reduce_fusion
  6.7 0.2 fusion.31
  6.9 0.7 iota_compare_fusion.1
  7.5 0.7 copy.50.table
  8.2 0.7 slice_bitcast_fusion.1
  8.9 1.5 fusion.20
  10.5 0.5 copy-done.8
  11.0 0.6 fusion.37
  11.7 0.3 fusion.8
  12.0 1.6 add_convert_fusion
  13.6 92.5 %dense.1 = (bf16[8,7168]{1,0:T(8,128)(2,1)}, bf16[2,2,576,256]{3,2,1,0:T(8,128)(2,1)}) custom-call(bf16[8,7168]{1,0:T(8,128)(2,1)} %stream.1, f32[1,7168]{1,0:T(1,128)} %bitcast.52, bf16[896,1152]{1,0:T(8,128)(2,1)} %wg.1, bf16[896,1152]{1,0:T(8,128)(2,1)} %wu.1, bf16[1152,896]{1,0:T(8,128)(2,1)} %wd.1, s32[9,2]{1,0:T(8,128)} %copy.50.table, ...), custom_call_target="tpu_custom_call" | custom-call | tf_op jit(solution)/shard_map/dense/pallas_call | solution.py:815
  106.1 93.2 %experts.1 = bf16[8,7168]{1,0:T(8,128)(2,1)} custom-call(bf16[8,7168]{1,0:T(8,128)(2,1)} %get-tuple-element.6.middle, f32[1,7168]{1,0:T(1,128)} %bitcast.53, s32[8,8]{1,0:T(8,128)} %ids.1, f32[8,8]{1,0:T(8,128)} %scores.1, bf16[7168,256]{1,0:T(8,128)(2,1)} %bitcast.45, bf16[7168,256]{1,0:T(8,128)(2,1)} %bitcast.46, bf16[256,7168]{1,0:T(8,128)(2,1)} %bitcast.47), custom_call_target="tpu_custom_call" | custom-call | tf_op jit(solution)/shard_map/experts/pallas_call | solution.py:421
  199.3 0.0 copy-start.6
  199.3 1.7 fusion.36
  201.0 0.7 multiply_maximum_fusion
  201.7 0.8 fusion.15
  202.6 0.5 fusion.5
  203.1 0.6 copy-done.2
  203.7 1.1 pad_maximum_fusion
  204.7 1.0 copy.83
  205.8 0.6 copy.84
  (22 shorter events, 0.1 us)
Async XLA Ops:
  8.9 1.6 copy-start.4
  8.9 1.6 copy-start
  8.9 2.1 %copy-start.8 = (bf16[6,256,576]{1,2,0:T(8,128)(2,1)S(1)}, bf16[6,256,576]{1,2,0:T(8,128)(2,1)}, u32[]{:S(2)}) copy-start(bf16[6,256,576]{1,2,0:T(8,128)(2,1)} %param.20) | copy-start | bytes 5308420
  199.3 3.2 %copy-start.5 = (f32[2,1,128]{2,1,0:T(1,128)S(1)}, f32[2,1,128]{2,1,0:T(1,128)}, u32[]{:S(2)}) copy-start(f32[2,1,128]{2,1,0:T(1,128)} %fusion.24) | copy-start | bytes 3076
  199.3 3.2 %copy-start.1 = (bf16[2,2,576,256]{3,2,1,0:T(8,128)(2,1)S(1)}, bf16[2,2,576,256]{3,2,1,0:T(8,128)(2,1)}, u32[]{:S(2)}) copy-start(bf16[2,2,576,256]{3,2,1,0:T(8,128)(2,1)} %get-tuple-element.5) | copy-start | bytes 3538948
  199.3 3.3 %copy-start.6 = (f32[2,512]{1,0:T(2,128)S(1)}, f32[2,512]{1,0:T(2,128)}, u32[]{:S(2)}) copy-start(f32[2,512]{1,0:T(2,128)} %slice_convert_fusion.1) | copy-start | bytes 12292
  199.3 3.3 %copy-start.7 = (pred[2,256]{1,0:T(4,128)(4,1)S(1)}, pred[2,256]{1,0:T(4,128)(4,1)}, u32[]{:S(2)}) copy-start(pred[2,256]{1,0:T(4,128)(4,1)} %iota_compare_fusion.1) | copy-start | bytes 1540
  202.5 1.1 copy-start.2
  204.7 1.0 copy-start.3

commit v6 on v5

--- a/solution.py
+++ b/solution.py
@@ -15,30 +15,6 @@
 
 EPS = 1e-06
 ROUTE_SCALE = 2.5
-
-
-def attend(queries, keys, lengths, newest):
-    scale = QKD ** (-0.5)
-    scores = jnp.einsum("rhl,rcl->rhc", queries, keys, preferred_element_type=jnp.float32) * scale
-    positions = jnp.arange(keys.shape[1])
-    valid = positions[None, None, :] < lengths[:, None, None]
-    masked = jnp.where(valid, scores, -1e30)
-    own_score = (
-        jnp.einsum("rhl,rl->rh", queries, newest, preferred_element_type=jnp.float32) * scale
-    )
-    top = jnp.maximum(jnp.max(masked, axis=-1), own_score)
-    expo = jnp.where(valid, jnp.exp(masked - top[..., None]), 0.0)
-    own_expo = jnp.exp(own_score - top)
-    total = jnp.sum(expo, axis=-1) + own_expo
-    weights = (expo / total[..., None]).astype(jnp.bfloat16)
-    own_weight = (own_expo / total).astype(jnp.bfloat16)
-    context = jnp.einsum(
-        "rhc,rcv->rhv", weights, keys[:, :, :VDIM], preferred_element_type=jnp.float32
-    )
-    context = context + own_weight.astype(jnp.float32)[..., None] * newest[:, None, :VDIM].astype(
-        jnp.float32
-    )
-    return context.astype(jnp.bfloat16)
 
 
 HALF = 3584
@@ -503,10 +479,11 @@
 
 
 def dense_kernel(
-    stream, gain, wg, wu, wd, table, leaving, middle, arrived,
+    stream, gain, wg, wu, wd, table, leaving, queries, resident, new_cols, new_rows, res_len, got_len,
+    middle, arrived, context,
     vg, vu, vd, nbuf, land, ft, gu, gx, gra, grb, grc, grd, hid, dn,
     pa, pb, pc, pd, qs, qx, fin, back,
-    held0, held1, far_out, far_in, near_out, near_in,
+    held0, held1, far_out, far_in, near_out, near_in, vq, vk,
     load_sem, send_sem, recv_sem,
 ):
     at, core, p, t = place()
@@ -516,7 +493,11 @@
         pltpu.make_async_copy(wd, vd, load_sem.at[2]),
         pltpu.make_async_copy(leaving.at[:, 0], held0.at[at[2]], load_sem.at[3]),
         pltpu.make_async_copy(leaving.at[:, 1], held1.at[at[1]], load_sem.at[4]),
+        pltpu.make_async_copy(queries, vq, load_sem.at[5]),
+        pltpu.make_async_copy(resident, vk, load_sem.at[6]),
     ]
+    loads[3].start()
+    loads[4].start()
     partner = device(at, 1 - core)
     line = [(lax.rem(p + q, 8), t) for q in range(1, 8)]
     greet(line + [device(beside(at, a, s), core) for a in (1, 2) for s in (1, 2, 3)])
@@ -527,14 +508,67 @@
     for o in range(8):
         nbuf[o] = normed[:, o * FD:(o + 1) * FD]
     sent = [wires.start(nbuf.at[peer[0]], land.at[p], peer) for peer in line]
-    for load in loads:
-        load.start()
     land[p] = nbuf[p]
+
+    loads[3].wait()
+    loads[4].wait()
+    held = (held0, held1)
+    ways, hops, on = [], [{}, {}], [{}, {}]
+    for l in (0, 1):
+        a1 = (2, 1)[l]
+        ways.append((device(beside(at, a1, 1), core), device(beside(at, a1, -1), core)))
+
+    def carry(l, item):
+        s = (at[(2, 1)[l]], item)
+        hops[l][item] = [wires.start(held[l].at[s], held[l].at[s], way) for way in ways[l]]
+
+    def relay_item(l, item):
+        hops[l][item][item].wait_recv()
+        s = (lax.rem(at[(2, 1)[l]] + (3, 1)[item], 4), item)
+        on[l][item] = wires.start(held[l].at[s], held[l].at[s], ways[l][item])
+
+    def settle(l):
+        hops[l][0][1].wait_recv()
+        hops[l][1][0].wait_recv()
+        on[l][0].wait_recv()
+        on[l][1].wait_recv()
+
+    for l in (0, 1):
+        carry(l, 0)
+    for n in (0, 1, 5, 6, 2):
+        loads[n].start()
 
     for copy in sent:
         copy.wait_recv()
     for x in range(4):
         ft[x // 2, x % 2, at[1], at[2]] = land[2 * x:2 * x + 2].reshape(16, FD).astype(jnp.bfloat16)
+
+    lane256 = lax.broadcasted_iota(jnp.int32, (128, 256), 1)
+    lane8 = lax.broadcasted_iota(jnp.int32, (128, 8), 1)
+    scale = QKD ** (-0.5)
+    cross_first = (((0,), (0,)), ((), ()))
+
+    def attend(r, keys, length):
+        query = vq[r]
+        scores = lax.dot_general(query, keys, cross_first, preferred_element_type=jnp.float32) * scale
+        newest = lax.dot_general(query, new_cols[...], cross_first, preferred_element_type=jnp.float32)
+        own = jnp.sum(jnp.where(lane8 == r, newest, 0.0), axis=1, keepdims=True) * scale
+        valid = lane256 < length
+        masked = jnp.where(valid, scores, -1e30)
+        top = jnp.maximum(jnp.max(masked, axis=1, keepdims=True), own)
+        expo = jnp.where(valid, jnp.exp(masked - top), 0.0)
+        own_expo = jnp.exp(own - top)
+        total = jnp.sum(expo, axis=1, keepdims=True) + own_expo
+        weights = (expo / total).astype(jnp.bfloat16)
+        own_weight = (own_expo / total).astype(jnp.bfloat16).astype(jnp.float32)
+        found = lax.dot_general(
+            weights, keys[0:VDIM], (((1,), (1,)), ((), ())), preferred_element_type=jnp.float32
+        )
+        context[r] = (found + own_weight * new_rows[pl.ds(r, 1), 0:VDIM]).astype(jnp.bfloat16)
+
+    def attend_stay(r, _):
+        attend(r, vk[r], res_len[r])
+        return _
 
     def spots(b, k, fixed):
         return (b, k) + tuple(fixed.get(a, slice(None)) for a in (1, 2))
@@ -574,25 +608,14 @@
             second[b, k, 2].near()
         for k in (0, 1):
             second[b, k, 0].relay()
+    loads[5].wait()
+    loads[6].wait()
+    lax.fori_loop(0, 2, attend_stay, 0)
     for b in (0, 1):
         for j in (3, 1, 2):
             for k in (0, 1):
                 second[b, k, j].relay()
-
-    loads[3].wait()
-    loads[4].wait()
-
-    held = (held0, held1)
-
-    def mover(l):
-        a1 = (2, 1)[l]
-
-        def index(step):
-            return (rem(a1, step),)
-
-        return Spread(wires, at, core, a1, held[l], index, (0,), (1,))
-
-    movers = [mover(0), mover(1)]
+    lax.fori_loop(2, 4, attend_stay, 0)
 
     def mine(l, step, slot):
         a1, a2 = ((2, 1), (1, 2))[l]
@@ -742,20 +765,23 @@
     for j in range(4):
         for k in (0, 1):
             second[1, k, j].finish()
-    for m in movers:
-        m.near()
+    for l in (0, 1):
+        carry(l, 1)
+    for l in (0, 1):
+        relay_item(l, 0)
     project(1)
     join(0)
     join(1)
+    for l in (0, 1):
+        relay_item(l, 1)
     gsums[0].relay()
-    for m in movers:
-        m.relay()
+    lax.fori_loop(4, 6, attend_stay, 0)
     gsums[1].relay()
-    activate(0)
-    for m in movers:
-        m.finish()
+    for l in (0, 1):
+        settle(l)
     for l in (0, 1):
         merge_far(l)
+    activate(0)
     for l in (0, 1):
         merge_near(l, 1, 0)
         merge_near(l, 0, 1)
@@ -774,6 +800,8 @@
         merge_end(l)
     dturn(0)
     dturn(1)
+    for slot in (0, 1):
+        attend(6 + slot, arrived[slot, 0], got_len[slot])
     dend(0)
     dend(1)
     sent = [wires.start(fin.at[peer[0]], back.at[p], peer) for peer in line]
@@ -786,7 +814,7 @@
     wires.close()
 
 
-def dense(stream, gain, wg, wu, wd, table, leaving):
+def dense(stream, gain, wg, wu, wd, table, leaving, queries, resident, new_cols, new_rows, res_len, got_len):
     vm, an = pl.BlockSpec(memory_space=pltpu.VMEM), pl.BlockSpec(memory_space=pl.ANY)
     sm = pl.BlockSpec(memory_space=pltpu.SMEM)
     bf, f32 = jnp.bfloat16, jnp.float32
@@ -810,22 +838,24 @@
         pltpu.VMEM((4, 2) + item, bf), pltpu.VMEM((4, 2) + item, bf),
         pltpu.VMEM((2, 2) + item, bf), pltpu.VMEM((2, 2) + item, bf),
         pltpu.VMEM((2, 2, 2) + item, bf), pltpu.VMEM((2, 2, 2) + item, bf),
-        pltpu.SemaphoreType.DMA((5,)), pltpu.SemaphoreType.DMA((240,)), pltpu.SemaphoreType.DMA((240,)),
+        pltpu.VMEM((8, 576, 128), bf), pltpu.VMEM((6, 576, 256), bf),
+        pltpu.SemaphoreType.DMA((7,)), pltpu.SemaphoreType.DMA((240,)), pltpu.SemaphoreType.DMA((240,)),
     ]
     return pl.pallas_call(
         dense_kernel,
         out_shape=(
             jax.ShapeDtypeStruct((8, 7168), bf),
             jax.ShapeDtypeStruct((2, 2) + item, bf),
+            jax.ShapeDtypeStruct((8, 128, 512), bf),
         ),
-        in_specs=[vm, vm, an, an, an, sm, an],
-        out_specs=(vm, vm),
+        in_specs=[vm, vm, an, an, an, sm, an, an, an, vm, vm, sm, sm],
+        out_specs=(vm, vm, vm),
         scratch_shapes=scratch,
         compiler_params=pltpu.CompilerParams(
             collective_id=2, has_side_effects=True, vmem_limit_bytes=67043328
         ),
         name="dense",
-    )(stream, gain, wg, wu, wd, table, leaving)
+    )(stream, gain, wg, wu, wd, table, leaving, queries, resident, new_cols, new_rows, res_len, got_len)
 
 
 def route(mig_dest, leave_len):
@@ -864,14 +894,12 @@
     gate_scores,
 ):
     table, moved_len = route(mig_dest, leave_len)
-    middle, moved = dense(
-        stream, dense_gain[None], w_gate, w_up, w_down, table, jnp.swapaxes(leaving, 2, 3)
+    middle, moved, context = dense(
+        stream, dense_gain[None], w_gate, w_up, w_down, table, jnp.swapaxes(leaving, 2, 3),
+        jnp.swapaxes(queries, 1, 2), jnp.swapaxes(resident, 1, 2), new_latent.T,
+        new_latent.astype(jnp.float32), res_len, moved_len,
     )
     arrived = jnp.swapaxes(moved, 2, 3)
-    stay = resident.shape[0]
-    context_stay = attend(queries[:stay], resident, res_len, new_latent[:stay])
-    context_moved = attend(queries[stay:], arrived[:, 0], moved_len, new_latent[stay:])
-    context = jnp.concatenate([context_stay, context_moved], axis=0)
     stream_out = moe(
         middle, moe_gain[None], expert_ids, gate_scores, expert_gate[0], expert_up[0], expert_down[0]
     )

time: 208 us -> 198 us (0.952)
  matrix products: 7.58 us -> 0 us
  other arithmetic: 6.07 us -> 2.32 us
    dot_general x6 -> x0, matrix products: 7.58 us -> none  [the longest x2 3.24 us: attend(): jnp.einsum('rhl,rl->rh', queries, newest, preferred_element_type=jnp.floa...]
    unnamed x20 -> x8, local copies, waits for them, and re-layouts: 2.82 us -> 5.53 us
where the time goes in v6:
time: 198 us; the launch traced here: 196 us
  Pallas kernels  186 us (94%)
  local copies, waits for them, and re-layouts  7.52 us (4%)
  other arithmetic  2.32 us (1%)
    pallas_call x1, Pallas kernels, moe(): pl.pallas_call(moe_kernel, out_shape=jax.ShapeDtypeStruct((8, 7168), bf),...  93.8 us
    pallas_call x1, Pallas kernels, dense(): pl.pallas_call(dense_kernel, out_shape=(jax.ShapeDtypeStruct((8, 7168), b...  92.1 us
    unnamed x8, local copies, waits for them, and re-layouts  5.53 us

profile of v6, /device:TPU:0, one launch (start us, length us, event | category | flops | bytes accessed | tf_op | source)
XLA Modules:
  0.0 196.5 jit_solution(11880396952040714361)
XLA Ops:
  0.7 0.1 pad_add_fusion.1
  0.7 0.8 constant_dynamic-slice_fusion
  1.5 0.1 copy.41
  1.6 0.1 broadcast_in_dim.51
  1.7 0.1 copy.39
  1.8 0.1 eq.32
  1.9 0.2 fusion
  2.1 0.2 slice_reduce_fusion
  2.3 0.7 fusion.2.got_len
  3.0 0.7 copy.42.table
  3.7 1.3 convert_element_type.3.new_rows
  5.0 1.5 copy.40
  6.5 92.1 %dense.1 = (bf16[8,7168]{1,0:T(8,128)(2,1)}, bf16[2,2,576,256]{3,2,1,0:T(8,128)(2,1)}, bf16[8,128,512]{2,1,0:T(8,128)(2,1)}) custom-call(bf16[8,7168]{1,0:T(8,128)(2,1)} %stream.1, f32[1,7168]{1,0:T(1,128)} %bitcast.21, bf16[896,1152]{1,0:T(8,128)(2,1)} %wg.1, bf16[896,1152]{1,0:T(8,128)(2,1)} %wu.1, bf16[1152,896]{1,0:T(8,128)(2,1)} %wd.1, ...), custom_call_target="tpu_custom_call" | custom-call | tf_op jit(solution)/shard_map/dense/pallas_call | solution.py:844
  98.6 93.8 %experts.1 = bf16[8,7168]{1,0:T(8,128)(2,1)} custom-call(bf16[8,7168]{1,0:T(8,128)(2,1)} %get-tuple-element.8.middle, f32[1,7168]{1,0:T(1,128)} %bitcast.22, s32[8,8]{1,0:T(8,128)} %ids.1, f32[8,8]{1,0:T(8,128)} %scores.1, bf16[7168,256]{1,0:T(8,128)(2,1)} %bitcast.13, bf16[7168,256]{1,0:T(8,128)(2,1)} %bitcast.14, bf16[256,7168]{1,0:T(8,128)(2,1)} %bitcast.15), custom_call_target="tpu_custom_call" | custom-call | tf_op jit(solution)/shard_map/experts/pallas_call | solution.py:397
  192.4 0.0 copy-start
  192.4 0.0 copy-start.1
  192.4 2.4 %copy.46 = bf16[8,128,512]{2,1,0:T(8,128)(2,1)} copy(bf16[8,128,512]{2,1,0:T(8,128)(2,1)} %get-tuple-element.18) | data formatting | bytes 2097152
  194.8 0.0 copy-done
  194.8 1.0 copy.47
  195.8 0.0 copy-done.1
  195.8 0.6 copy.48
  (2 shorter events, 0.0 us)
Async XLA Ops:
  192.4 2.4 %copy-start = (bf16[2,2,576,256]{3,2,1,0:T(8,128)(2,1)S(1)}, bf16[2,2,576,256]{3,2,1,0:T(8,128)(2,1)}, u32[]{:S(2)}) copy-start(bf16[2,2,576,256]{3,2,1,0:T(8,128)(2,1)} %get-tuple-element.7) | copy-start | bytes 3538948
  192.4 3.4 %copy-start.1 = (bf16[8,7168]{1,0:T(8,128)(2,1)S(1)}, bf16[8,7168]{1,0:T(8,128)(2,1)}, u32[]{:S(2)}) copy-start(bf16[8,7168]{1,0:T(8,128)(2,1)} %experts.1) | copy-start | bytes 344068

commit v7 on v6

--- a/solution.py
+++ b/solution.py
@@ -213,6 +213,10 @@
         for k in range(3):
             fixed, pair = third[k][n]
             last[k].append(forward(k, ORDERS[k][2], fixed, pair))
+        if n == 1:
+            for k in range(3):
+                across[k][0].wait_recv()
+                product(ot, 1 - core, k, 0, False)
     for k in range(3):
         hand(k, 1)
         hand(k, 3)
@@ -224,15 +228,15 @@
 
     lax.fori_loop(0, 2, side, 0)
     for k in range(3):
-        for step in (0, 1, 3):
+        for step in (1, 3):
             across[k][step].wait_recv()
 
     def side_other(n, _):
         for k in range(3):
-            product(ot, 1 - core, k, n + n // 2, False)
+            product(ot, 1 - core, k, 2 * n + 1, False)
         return _
 
-    lax.fori_loop(0, 3, side_other, 0)
+    lax.fori_loop(0, 2, side_other, 0)
     tails = [[], [], []]
     for n in range(4):
         for k in range(3):
@@ -479,7 +483,7 @@
 
 
 def dense_kernel(
-    stream, gain, wg, wu, wd, table, leaving, queries, resident, new_cols, new_rows, res_len, got_len,
+    stream, gain, wg, wu, wd, table, leaving, queries, resident, new_rows, res_len, got_len,
     middle, arrived, context,
     vg, vu, vd, nbuf, land, ft, gu, gx, gra, grb, grc, grd, hid, dn,
     pa, pb, pc, pd, qs, qx, fin, back,
@@ -545,13 +549,14 @@
 
     lane256 = lax.broadcasted_iota(jnp.int32, (128, 256), 1)
     lane8 = lax.broadcasted_iota(jnp.int32, (128, 8), 1)
+    sub8 = lax.broadcasted_iota(jnp.int32, (8, VDIM), 0)
     scale = QKD ** (-0.5)
     cross_first = (((0,), (0,)), ((), ()))
 
     def attend(r, keys, length):
         query = vq[r]
         scores = lax.dot_general(query, keys, cross_first, preferred_element_type=jnp.float32) * scale
-        newest = lax.dot_general(query, new_cols[...], cross_first, preferred_element_type=jnp.float32)
+        newest = jnp.dot(new_rows[...], query, preferred_element_type=jnp.float32).T
         own = jnp.sum(jnp.where(lane8 == r, newest, 0.0), axis=1, keepdims=True) * scale
         valid = lane256 < length
         masked = jnp.where(valid, scores, -1e30)
@@ -564,7 +569,9 @@
         found = lax.dot_general(
             weights, keys[0:VDIM], (((1,), (1,)), ((), ())), preferred_element_type=jnp.float32
         )
-        context[r] = (found + own_weight * new_rows[pl.ds(r, 1), 0:VDIM]).astype(jnp.bfloat16)
+        row = new_rows[:, 0:VDIM].astype(jnp.float32)
+        row = jnp.sum(jnp.where(sub8 == r, row, 0.0), axis=0, keepdims=True)
+        context[r] = (found + own_weight * row).astype(jnp.bfloat16)
 
     def attend_stay(r, _):
         attend(r, vk[r], res_len[r])
@@ -814,7 +821,7 @@
     wires.close()
 
 
-def dense(stream, gain, wg, wu, wd, table, leaving, queries, resident, new_cols, new_rows, res_len, got_len):
+def dense(stream, gain, wg, wu, wd, table, leaving, queries, resident, new_rows, res_len, got_len):
     vm, an = pl.BlockSpec(memory_space=pltpu.VMEM), pl.BlockSpec(memory_space=pl.ANY)
     sm = pl.BlockSpec(memory_space=pltpu.SMEM)
     bf, f32 = jnp.bfloat16, jnp.float32
@@ -848,14 +855,14 @@
             jax.ShapeDtypeStruct((2, 2) + item, bf),
             jax.ShapeDtypeStruct((8, 128, 512), bf),
         ),
-        in_specs=[vm, vm, an, an, an, sm, an, an, an, vm, vm, sm, sm],
+        in_specs=[vm, vm, an, an, an, sm, an, an, an, vm, sm, sm],
         out_specs=(vm, vm, vm),
         scratch_shapes=scratch,
         compiler_params=pltpu.CompilerParams(
             collective_id=2, has_side_effects=True, vmem_limit_bytes=67043328
         ),
         name="dense",
-    )(stream, gain, wg, wu, wd, table, leaving, queries, resident, new_cols, new_rows, res_len, got_len)
+    )(stream, gain, wg, wu, wd, table, leaving, queries, resident, new_rows, res_len, got_len)
 
 
 def route(mig_dest, leave_len):
@@ -896,8 +903,8 @@
     table, moved_len = route(mig_dest, leave_len)
     middle, moved, context = dense(
         stream, dense_gain[None], w_gate, w_up, w_down, table, jnp.swapaxes(leaving, 2, 3),
-        jnp.swapaxes(queries, 1, 2), jnp.swapaxes(resident, 1, 2), new_latent.T,
-        new_latent.astype(jnp.float32), res_len, moved_len,
+        jnp.swapaxes(queries, 1, 2), jnp.swapaxes(resident, 1, 2), new_latent,
+        res_len, moved_len,
     )
     arrived = jnp.swapaxes(moved, 2, 3)
     stream_out = moe(

time: 198 us -> 194 us (0.980)
  Pallas kernels: 186 us -> 184 us
    unnamed x8 -> x7, local copies, waits for them, and re-layouts: 5.53 us -> 4.03 us
where the time goes in v7:
time: 194 us; the launch traced here: 192 us
  Pallas kernels  184 us (95%)
  local copies, waits for them, and re-layouts  6.02 us (3%)
    pallas_call x1, Pallas kernels, moe(): pl.pallas_call(moe_kernel, out_shape=jax.ShapeDtypeStruct((8, 7168), bf),...  92.3 us
    pallas_call x1, Pallas kernels, dense(): pl.pallas_call(dense_kernel, out_shape=(jax.ShapeDtypeStruct((8, 7168), b...  91.8 us
    unnamed x7, local copies, waits for them, and re-layouts  4.03 us

profile of v7, /device:TPU:0, one launch (start us, length us, event | category | flops | bytes accessed | tf_op | source)
XLA Modules:
  0.0 191.8 jit_solution(6532229420666136416)
XLA Ops:
  0.7 0.1 pad_add_fusion.1
  0.7 0.8 constant_dynamic-slice_fusion
  1.5 0.1 copy.36
  1.6 0.1 broadcast_in_dim.51
  1.7 0.1 copy.35
  1.8 0.1 eq.32
  1.9 0.2 fusion
  2.1 0.2 slice_reduce_fusion
  2.3 0.7 fusion.2.got_len
  3.0 0.7 copy.37.table
  3.6 91.8 %dense.1 = (bf16[8,7168]{1,0:T(8,128)(2,1)}, bf16[2,2,576,256]{3,2,1,0:T(8,128)(2,1)}, bf16[8,128,512]{2,1,0:T(8,128)(2,1)}) custom-call(bf16[8,7168]{1,0:T(8,128)(2,1)} %stream.1, f32[1,7168]{1,0:T(1,128)} %bitcast.19, bf16[896,1152]{1,0:T(8,128)(2,1)} %wg.1, bf16[896,1152]{1,0:T(8,128)(2,1)} %wu.1, bf16[1152,896]{1,0:T(8,128)(2,1)} %wd.1, ...), custom_call_target="tpu_custom_call" | custom-call | tf_op jit(solution)/shard_map/dense/pallas_call | solution.py:851
  95.5 92.3 %experts.1 = bf16[8,7168]{1,0:T(8,128)(2,1)} custom-call(bf16[8,7168]{1,0:T(8,128)(2,1)} %get-tuple-element.8.middle, f32[1,7168]{1,0:T(1,128)} %bitcast.20, s32[8,8]{1,0:T(8,128)} %ids.1, f32[8,8]{1,0:T(8,128)} %scores.1, bf16[7168,256]{1,0:T(8,128)(2,1)} %bitcast.12, bf16[7168,256]{1,0:T(8,128)(2,1)} %bitcast.13, bf16[256,7168]{1,0:T(8,128)(2,1)} %bitcast.14), custom_call_target="tpu_custom_call" | custom-call | tf_op jit(solution)/shard_map/experts/pallas_call | solution.py:401
  187.8 0.0 copy-start
  187.8 0.0 copy-start.1
  187.8 2.4 %copy.41 = bf16[8,128,512]{2,1,0:T(8,128)(2,1)} copy(bf16[8,128,512]{2,1,0:T(8,128)(2,1)} %get-tuple-element.18) | data formatting | bytes 2097152
  190.1 0.0 copy-done
  190.1 1.0 copy.42
  191.2 0.0 copy-done.1
  191.2 0.6 copy.43
  (2 shorter events, 0.0 us)
Async XLA Ops:
  187.8 2.4 %copy-start = (bf16[2,2,576,256]{3,2,1,0:T(8,128)(2,1)S(1)}, bf16[2,2,576,256]{3,2,1,0:T(8,128)(2,1)}, u32[]{:S(2)}) copy-start(bf16[2,2,576,256]{3,2,1,0:T(8,128)(2,1)} %get-tuple-element.7) | copy-start | bytes 3538948
  187.8 3.4 %copy-start.1 = (bf16[8,7168]{1,0:T(8,128)(2,1)S(1)}, bf16[8,7168]{1,0:T(8,128)(2,1)}, u32[]{:S(2)}) copy-start(bf16[8,7168]{1,0:T(8,128)(2,1)} %experts.1) | copy-start | bytes 344068
